TPU v7x, 32 devices: a whole 2x2x4 slice. The times are simulated.
32 devices in a mesh: section: 4 (over z), tensor: 8 (over y, x, core).
Axes of the slice: x: 2, y: 2, z: 4, core: 2. Of those that a mesh axis runs over, the one named last changes fastest.
Arguments:
- hidden: bfloat16 [32, 8192], P('section', 'tensor'), may hold values from -33 to 33, as said below
- out_weight: bfloat16 [4096, 8192], P(('section', 'tensor')), may hold values from -12 to 12, as said below
- targets: int32 [32], replicated, may hold values from 0 to 4095
- token_mask: int32 [32], replicated, may hold values 0 or 1
Outputs:
- ce_loss: float32 [], replicated
- z_loss: float32 [], replicated
- grad_hidden: float32 [32, 8192], P('section', 'tensor')
- grad_weight: bfloat16 [4096, 8192], P(('section', 'tensor'))
Inputs may be any that keep to these rules, and one draw needn't show every extreme that they name: hidden rows of one token have one scale; entries are bounded. `out_weight`: entries are bounded.
All inputs are finite; a program needn't handle non-finite values.
Results may differ from a plain program's by a relative error of at most 0.0026.
Values may be sent and summed in bfloat16 or wider, within the bound.
No kernel may reach another device: no remote copies, remote signals or barrier semaphores. Data moves between devices by JAX's collectives and lax.ppermute only.
A program may use at most 64 MiB of HBM per device.

v0:
```python
import jax
import jax.numpy as jnp
from jax import lax
from jax.sharding import PartitionSpec as P

z_weight = 0.0001


def body(hidden, out_weight, targets, token_mask):
    vocab_dev = out_weight.shape[0]
    full_rows = lax.all_gather(hidden, "tensor", axis=1, tiled=True)
    gathered = lax.all_gather(full_rows, "section", axis=0, tiled=True)
    token_count = gathered.shape[0]
    logits = lax.dot_general(
        gathered, out_weight, (((1,), (1,)), ((), ())), preferred_element_type=jnp.float32
    )
    vocab_start = (
        lax.axis_index("section") * lax.axis_size("tensor") + lax.axis_index("tensor")
    ) * vocab_dev
    local_ids = targets - vocab_start
    target_hit = local_ids[:, None] == jnp.arange(vocab_dev, dtype=jnp.int32)[None, :]
    picked_local = jnp.sum(jnp.where(target_hit, logits, 0.0), axis=1)
    local_top = jnp.max(logits, axis=1)
    row_top = lax.pmax(local_top, ("section", "tensor"))
    local_total = jnp.sum(jnp.exp(logits - row_top[:, None]), axis=1)
    row_total, picked = lax.psum((local_total, picked_local), ("section", "tensor"))
    log_total = row_top + jnp.log(row_total)
    kept = token_mask.astype(jnp.float32)
    ce_loss = jnp.sum(kept * (log_total - picked)) / token_count
    z_loss = jnp.sum(kept * log_total * log_total) / token_count
    factor = 1.0 + 2.0 * z_weight * log_total
    probs = jnp.exp(logits - log_total[:, None])
    dlogits = (kept[:, None] * (factor[:, None] * probs - target_hit.astype(jnp.float32))).astype(
        jnp.bfloat16
    )
    grad_weight = lax.dot_general(
        dlogits, gathered, (((0,), (0,)), ((), ())), preferred_element_type=jnp.float32
    ).astype(jnp.bfloat16)
    width_part = lax.psum_scatter(
        lax.dot_general(
            out_weight, dlogits, (((0,), (1,)), ((), ())), preferred_element_type=jnp.float32
        ),
        "tensor",
        scatter_dimension=0,
        tiled=True,
    )
    mine = lax.psum_scatter(width_part, "section", scatter_dimension=1, tiled=True)
    grad_hidden = mine.T
    return (ce_loss, z_loss, grad_hidden, grad_weight)


def solution(mesh):
    placed = (P("section", "tensor"), P(("section", "tensor"), None), P(), P())
    return jax.shard_map(
        body,
        mesh=mesh,
        in_specs=placed,
        out_specs=(P(), P(), P("section", "tensor"), P(("section", "tensor"), None)),
        check_vma=False,
    )
```

profile of v0, /device:TPU:0, one launch (start us, length us, event | category | flops | bytes accessed | tf_op | source)
XLA Modules:
  0.0 185.8 jit_solution(5926214995159261907)
XLA Ops:
  7.2 0.0 copy-start
  7.2 0.0 copy-start.2
  7.2 0.0 reduce-scatter.3.cloned.1.call-start
  7.2 0.8 convert_element_type.12
  8.0 10.9 %all_gather.6 = bf16[8,8192]{1,0:T(8,128)(2,1)S(1)} all-gather(bf16[8,1024]{1,0:T(8,128)(2,1)} %param.4), channel_id=1, replica_groups=mesh['section'=4,'tensor'=8] {'tensor'}, dimensions={1}, use_global_device_ids=true | all-gather | bytes 147456 | tf_op jit(solution)/shard_map/all_gather | solution.py:11
  18.9 16.3 %all_gather.7 = bf16[32,8192]{1,0:T(8,128)(2,1)S(1)} all-gather(bf16[8,8192]{1,0:T(8,128)(2,1)S(1)} %all_gather.6), channel_id=1, replica_groups=mesh['section'=4,'tensor'=8] {'section'}, dimensions={0}, use_global_device_ids=true | all-gather | bytes 655360 | tf_op jit(solution)/shard_map/all_gather | solution.py:12
  35.2 0.0 copy-done
  35.2 0.9 fusion.1
  36.1 39.6 %pmax.7 = f32[32]{0:T(128)S(1)} all-reduce(f32[32]{0:T(128)S(1)} %get-tuple-element.12), channel_id=1, replica_groups=mesh['section'=4,'tensor'=8] {'section','tensor'}, use_global_device_ids=true, to_apply=%region_1.2 | all-reduce | flops 32 | bytes 256 | tf_op jit(solution)/shard_map/pmax | solution.py:24
  75.7 0.0 copy-done.2
  75.7 0.2 select_reduce_fusion
  75.9 41.0 %all-reduce = (f32[32]{0:T(128)S(1)}, f32[32]{0:T(128)S(1)}) all-reduce(f32[32]{0:T(128)S(1)} %get-tuple-element.5, f32[32]{0:T(128)S(1)} %get-tuple-element.4), channel_id=1, replica_groups=mesh['section'=4,'tensor'=8] {'section','tensor'}, use_global_device_ids=true, to_apply=%region_3.4 | all-reduce | flops 64 | bytes 512 | tf_op jit(solution)/shard_map/psum | solution.py:26
  116.9 0.0 copy-start.1
  116.9 1.4 convolution_bitcast_fusion
  118.3 0.0 reduce-scatter.3.cloned.1.call-update
  118.4 0.0 reduce-scatter.5.cloned.1.call-start
  118.4 0.0 copy-done.1
  118.4 0.6 fusion
  120.3 34.1 %reduce-scatter.3.cloned.1.call-done = f32[1024,32]{0,1:T(8,128)} async-done(((f32[8192,32]{0,1:T(8,128)}), f32[1024,32]{0,1:T(8,128)}) %reduce-scatter.3.cloned.1.call-update) | async-done | bytes 131088 | tf_op jit(solution)/shard_map/reduce_scatter | solution.py:39
  154.4 0.0 reduce-scatter.5.cloned.1.call-update
  154.4 2.1 %convolution_convert_fusion = bf16[128,8192]{1,0:T(8,128)(2,1)} fusion(bf16[32,8192]{1,0:T(8,128)(2,1)S(1)} %all_gather.7, f32[32,128]{1,0:T(8,128)S(1)} %get-tuple-element.13, f32[32]{0:T(128)S(1)} %get-tuple-element.11, f32[32]{0:T(128)S(1)} %get-tuple-element.10, f32[32]{0:T(128)S(1)} %convert_element_type.12, s32[32]{0:T(128)S(1)} %broadcast_subtract_fusion), kind=kOutput, calls=%fused_computation | convolution fusion | flops 68186112 | bytes 2638336 | tf_op jit(solution)/shard_map/dot_general | solution.py:36
  156.6 20.1 %reduce-scatter.5.cloned.1.call-done = f32[1024,8]{0,1:T(8,128)} async-done(((f32[1024,32]{0,1:T(8,128)}), f32[1024,8]{0,1:T(8,128)}) %reduce-scatter.5.cloned.1.call-update) | async-done | bytes 32784 | tf_op jit(solution)/shard_map/reduce_scatter | solution.py:47
  (2 shorter events, 0.0 us)
Async XLA Ops:
  7.2 28.1 %copy-start = (bf16[128,8192]{1,0:T(8,128)(2,1)S(1)}, bf16[128,8192]{1,0:T(8,128)(2,1)}, u32[]{:S(2)}) copy-start(bf16[128,8192]{1,0:T(8,128)(2,1)} %param.5) | copy-start | bytes 6291460
  7.2 68.5 %copy-start.2 = (s32[32]{0:T(128)S(1)}, s32[32]{0:T(128)}, u32[]{:S(2)}) copy-start(s32[32]{0:T(128)} %param.6) | copy-start | bytes 388
  7.2 147.2 %reduce-scatter.3.cloned.1.call-start = ((), (), s32[]{:S(2)}) async-start(), calls=%async_computation.2 | async-start | bytes 1179648 | tf_op jit(solution)/shard_map/reduce_scatter | solution.py:39
  116.9 1.5 copy-start.1
  118.4 58.3 %reduce-scatter.5.cloned.1.call-start = ((), (), s32[]{:S(2)}) async-start(), calls=%async_computation.3 | async-start | bytes 163840 | tf_op jit(solution)/shard_map/reduce_scatter | solution.py:47
Sparse Core Ops, SparseCore 0:
  118.5 35.8 reduce-scatter.2
  157.2 19.4 reduce-scatter.4
where the time goes:
time: 186 us
  blocking collectives  108 us (58%)
  waiting for transfers between devices  54.2 us (29%)
  between operations  17.6 us (9%)
  matrix products  4.48 us (2%)
    psum x1, blocking collectives, body(): lax.psum((local_total, picked_local), ('section', 'tensor'))  41 us
    pmax x1, blocking collectives, body(): row_top = lax.pmax(local_top, ('section', 'tensor'))  39.6 us
    reduce_scatter x1, waiting for transfers between devices, body(): lax.psum_scatter(lax.dot_general(out_weight, dlogits, (((0,), (1,)), ((),...  34.1 us
    reduce_scatter x1, waiting for transfers between devices, body(): lax.psum_scatter(width_part, 'section', scatter_dimension=1, tiled=True)  20.1 us
    all_gather x1, blocking collectives, body(): gathered = lax.all_gather(full_rows, 'section', axis=0, tiled=True)  16.3 us
    all_gather x1, blocking collectives, body(): full_rows = lax.all_gather(hidden, 'tensor', axis=1, tiled=True)  10.9 us
  transfers between devices with their start and end apart: 2, of which 2 were waited for; matrix products, arithmetic and copies ran while one was open for 1% of the time, Pallas kernels for 0%

commit v1 on v0

v1 whole, which is shorter than its diff:
```python
import jax
import jax.numpy as jnp
from jax import lax
from jax.sharding import PartitionSpec as P

z_weight = 0.0001
BOTH = ("section", "tensor")


def body(hidden, out_weight, targets, token_mask):
    sections, tensors = lax.axis_size("section"), lax.axis_size("tensor")
    devices = sections * tensors
    vocab_dev = out_weight.shape[0]
    rows, block = hidden.shape
    half = block // 2
    token_count = sections * rows
    core = lax.axis_index("tensor") % 2
    swap = [(i, i ^ 1) for i in range(tensors)]

    halves = hidden.reshape(rows, 2, half).transpose(1, 0, 2)
    sent = jnp.broadcast_to(halves[None], (devices // 2, 2, rows, half)).reshape(devices, rows, half)
    mine = lax.all_to_all(sent, BOTH, 0, 0)
    other = lax.ppermute(mine, "tensor", swap)
    low = jnp.where(core == 0, mine, other)
    high = jnp.where(core == 0, other, mine)
    gathered = jnp.stack([low, high], axis=2).reshape(sections, tensors, rows, 2, half)
    gathered = gathered.transpose(0, 2, 1, 3, 4).reshape(token_count, tensors * block)

    logits = lax.dot_general(
        gathered, out_weight, (((1,), (1,)), ((), ())), preferred_element_type=jnp.float32
    )
    vocab_start = (lax.axis_index("section") * tensors + lax.axis_index("tensor")) * vocab_dev
    local_ids = targets - vocab_start
    target_hit = local_ids[:, None] == jnp.arange(vocab_dev, dtype=jnp.int32)[None, :]
    picked_local = jnp.sum(jnp.where(target_hit, logits, 0.0), axis=1)
    local_top = jnp.max(logits, axis=1)
    local_total = jnp.sum(jnp.exp(logits - local_top[:, None]), axis=1)

    stats = jnp.concatenate([local_top, local_total, picked_local])
    width = -(-stats.shape[0] // 128) * 128
    stats = jnp.pad(stats, (0, width - stats.shape[0]))
    stats = jnp.broadcast_to(stats, (devices, 1, width))
    stats = lax.all_to_all(stats, BOTH, 0, 0).reshape(devices, width)
    tops = stats[:, :token_count]
    totals = stats[:, token_count : 2 * token_count]
    picked = jnp.sum(stats[:, 2 * token_count : 3 * token_count], axis=0)
    row_top = jnp.max(tops, axis=0)
    row_total = jnp.sum(totals * jnp.exp(tops - row_top[None, :]), axis=0)
    log_total = row_top + jnp.log(row_total)

    kept = token_mask.astype(jnp.float32)
    ce_loss = jnp.sum(kept * (log_total - picked)) / token_count
    z_loss = jnp.sum(kept * log_total * log_total) / token_count
    factor = 1.0 + 2.0 * z_weight * log_total
    probs = jnp.exp(logits - log_total[:, None])
    dlogits = (kept[:, None] * (factor[:, None] * probs - target_hit.astype(jnp.float32))).astype(
        jnp.bfloat16
    )
    grad_weight = lax.dot_general(
        dlogits, gathered, (((0,), (0,)), ((), ())), preferred_element_type=jnp.float32
    ).astype(jnp.bfloat16)

    partial = lax.dot_general(
        dlogits, out_weight, (((1,), (0,)), ((), ())), preferred_element_type=jnp.float32
    ).reshape(sections, rows, tensors, 2, half)
    first, second = partial[:, :, :, 0], partial[:, :, :, 1]
    given = jnp.where(core == 0, second, first)
    pair = jnp.where(core == 0, first, second) + lax.ppermute(given, "tensor", swap)
    pair = pair.astype(jnp.bfloat16).transpose(0, 2, 1, 3).reshape(devices, rows, half)
    shares = lax.all_to_all(pair, BOTH, 0, 0).reshape(devices // 2, 2, rows, half)
    grad_hidden = jnp.sum(shares.astype(jnp.float32), axis=0).transpose(1, 0, 2).reshape(rows, block)
    return (ce_loss, z_loss, grad_hidden, grad_weight)


def solution(mesh):
    placed = (P("section", "tensor"), P(("section", "tensor"), None), P(), P())
    return jax.shard_map(
        body,
        mesh=mesh,
        in_specs=placed,
        out_specs=(P(), P(), P("section", "tensor"), P(("section", "tensor"), None)),
        check_vma=False,
    )
```

time: 186 us -> 53.3 us (0.29)
  blocking collectives: 108 us -> 17.7 us
  waiting for transfers between devices: 54.2 us -> 16.4 us
  between operations: 17.6 us -> 4.31 us
  starting transfers between devices: 0.08 us -> 5.2 us
  local copies, waits for them, and re-layouts: 0.02 us -> 2.46 us
    reduce_scatter x2 -> x0, waiting for transfers between devices: 54.2 us -> none  [the longest x1 34.1 us: body(): lax.psum_scatter(lax.dot_general(out_weight, dlogits, (((0,), (1,)), ((),...]
    psum x1 -> x0, blocking collectives: 41 us -> none  [body(): lax.psum((local_total, picked_local), ('section', 'tensor'))]
    pmax x1 -> x0, blocking collectives: 39.6 us -> none  [body(): row_top = lax.pmax(local_top, ('section', 'tensor'))]
    all_gather x2 -> x0, blocking collectives: 27.2 us -> none  [the longest x1 16.3 us: body(): gathered = lax.all_gather(full_rows, 'section', axis=0, tiled=True)]
    all_to_all x0 -> x1, blocking collectives: none -> 17.7 us  [body(): mine = lax.all_to_all(sent, BOTH, 0, 0)]
    all_to_all x0 -> x2, waiting for transfers between devices: none -> 13.6 us  [the longest x1 7.08 us: body(): stats = lax.all_to_all(stats, BOTH, 0, 0).reshape(devices, width)]
    all_to_all x0 -> x2, starting transfers between devices: none -> 5.13 us  [the longest x1 2.58 us: body(): lax.all_to_all(pair, BOTH, 0, 0).reshape(devices // 2, 2, rows, half)]
    ppermute x0 -> x2, waiting for transfers between devices: none -> 2.77 us  [the longest x1 1.9 us: body(): lax.ppermute(given, 'tensor', swap)]
  transfers between devices with their start and end apart: 2 -> 4, of which waited for: 2 -> 4; matrix products, arithmetic and copies ran while one was open for 1% -> 6% of each run, Pallas kernels for 0% -> 0%
where the time goes in v1:
time: 53.3 us; the launch traced here: 52.9 us
  blocking collectives  17.7 us (33%)
  waiting for transfers between devices  16.4 us (31%)
  starting transfers between devices  5.2 us (10%)
  between operations  4.31 us (8%)
  matrix products  3.51 us (7%)
  other arithmetic  3.31 us (6%)
  local copies, waits for them, and re-layouts  2.46 us (5%)
    all_to_all x1, blocking collectives, body(): mine = lax.all_to_all(sent, BOTH, 0, 0)  17.7 us
    all_to_all x1, waiting for transfers between devices, body(): stats = lax.all_to_all(stats, BOTH, 0, 0).reshape(devices, width)  7.08 us
    all_to_all x1, waiting for transfers between devices, body(): lax.all_to_all(pair, BOTH, 0, 0).reshape(devices // 2, 2, rows, half)  6.54 us
    all_to_all x1, starting transfers between devices, body(): lax.all_to_all(pair, BOTH, 0, 0).reshape(devices // 2, 2, rows, half)  2.58 us
    all_to_all x1, starting transfers between devices, body(): stats = lax.all_to_all(stats, BOTH, 0, 0).reshape(devices, width)  2.54 us
    dot_general x1, matrix products, body(): lax.dot_general(dlogits, gathered, (((0,), (0,)), ((), ())), preferred_el...  2.13 us
    ppermute x1, waiting for transfers between devices, body(): lax.ppermute(given, 'tensor', swap)  1.9 us
  transfers between devices with their start and end apart: 4, of which 4 were waited for; matrix products, arithmetic and copies ran while one was open for 6% of the time, Pallas kernels for 0%

profile of v1, /device:TPU:0, one launch (start us, length us, event | category | flops | bytes accessed | tf_op | source)
XLA Modules:
  0.0 52.9 jit_solution(7188493800839651923)
XLA Ops:
  0.6 0.0 copy-start
  0.6 0.9 %broadcast_in_dim.8 = bf16[16,2,8,512]{3,2,1,0:T(8,128)(2,1)S(1)} broadcast(bf16[2,8,512]{2,1,0:T(8,128)(2,1)} %bitcast.53), dimensions={1,2,3} | broadcast | bytes 278528 | tf_op jit(solution)/shard_map/broadcast_in_dim | solution.py:21
  1.5 17.7 %all_to_all.15 = bf16[32,8,512]{2,1,0:T(8,128)(2,1)S(1)} all-to-all(bf16[32,8,512]{2,1,0:T(8,128)(2,1)S(1)} %bitcast.47), channel_id=1, replica_groups=mesh['section'=4,'tensor'=8] {'section','tensor'}, dimensions={0} | all-to-all | bytes 524288 | tf_op jit(solution)/shard_map/all_to_all | solution.py:22
  19.2 0.0 collective-permute-start
  19.2 0.7 %broadcast_subtract_fusion = s32[32]{0:T(128)S(1)} fusion(s32[32]{0:T(128)} %param.6, s32[]{:T(128)S(6)} %mul.45), kind=kLoop, calls=%fused_computation.26 | loop fusion | flops 32 | bytes 260 | tf_op jit(solution)/shard_map/sub | solution.py:33
  19.9 0.9 %collective-permute-done = bf16[32,8,512]{2,1,0:T(8,128)(2,1)S(1)} collective-permute-done((bf16[32,8,512]{2,1,0:T(8,128)(2,1)S(1)}, bf16[32,8,512]{2,1,0:T(8,128)(2,1)S(1)}, u32[]{:S(2)}, u32[]{:S(2)}) %collective-permute-start) | collective-permute-done | bytes 262176 | tf_op jit(solution)/shard_map/ppermute | solution.py:23
  20.8 0.1 maximum_bitcast_fusion
  20.9 0.5 %copy.26 = bf16[4,8,8,2,512]{4,3,2,1,0:T(2,128)(2,1)S(1)} copy(bf16[4,8,8,2,512]{4,1,2,0,3:T(8,128)(2,1)S(1)} %maximum_bitcast_fusion) | data formatting | bytes 1048576 | tf_op jit(solution)/shard_map/transpose | solution.py:27
  21.4 0.0 copy-start.1
  21.4 0.4 reshape.60
  21.8 0.0 copy-done
  21.8 0.9 %fusion.6 = (f32[32]{0:T(128)S(1)}, f32[32,128]{1,0:T(8,128)S(1)}) fusion(bf16[32,8192]{1,0:T(8,128)(2,1)S(1)} %reshape.60, bf16[128,8192]{1,0:T(8,128)(2,1)S(1)} %copy-done), kind=kOutput, calls=%fused_computation.28 | convolution fusion | flops 67112928 | bytes 2637952 | tf_op jit(solution)/shard_map/dot_general | solution.py:29
  22.8 0.2 exponential_reduce_fusion
  23.0 0.1 select_maximum_fusion
  23.0 0.6 %broadcast_in_dim.10 = f32[32,1,128]{2,1,0:T(1,128)} broadcast(f32[128]{0:T(128)S(1)} %select_maximum_fusion), dimensions={2} | broadcast | bytes 16896 | tf_op jit(solution)/shard_map/broadcast_in_dim | solution.py:42
  23.7 2.5 %all-to-all-start.1 = ((f32[32,1,128]{2,1,0:T(1,128)}), f32[32,1,128]{2,1,0:T(1,128)S(1)}, u32[]{:S(2)}, u32[]{:S(2)}) async-start(f32[32,1,128]{2,1,0:T(1,128)} %broadcast_in_dim.10), calls=%async_computation.1 | async-start | bytes 32768 | tf_op jit(solution)/shard_map/all_to_all | solution.py:43
  26.2 0.0 copy-done.1
  26.2 7.1 %all-to-all-done.1 = f32[32,1,128]{2,1,0:T(1,128)S(1)} async-done(((f32[32,1,128]{2,1,0:T(1,128)}), f32[32,1,128]{2,1,0:T(1,128)S(1)}, u32[]{:S(2)}, u32[]{:S(2)}) %all-to-all-start.1) | async-done | bytes 16416 | tf_op jit(solution)/shard_map/all_to_all | solution.py:43
  33.3 0.1 slice_reduce_fusion
  33.5 0.5 fusion.5
  33.9 0.1 select_bitcast_fusion
  34.0 0.1 collective-permute-start.1
  34.1 1.9 %collective-permute-done.1 = f32[4,8,8,512]{3,1,2,0:T(8,128)S(1)} collective-permute-done((f32[4,8,8,512]{3,1,2,0:T(8,128)S(1)}, f32[4,8,8,512]{3,1,2,0:T(8,128)S(1)}, u32[]{:S(2)}, u32[]{:S(2)}) %collective-permute-start.1) | collective-permute-done | bytes 524320 | tf_op jit(solution)/shard_map/ppermute | solution.py:68
  36.0 0.8 %fusion.2 = bf16[4,8,8,512]{3,1,2,0:T(8,128)(2,1)} fusion(f32[4,8,8,512]{3,1,2,0:T(8,128)S(1)} %collective-permute-done.1, f32[4,8,8,2,512]{4,1,3,2,0:T(8,128)S(1)} %bitcast.45, pred[]{:T(512)S(6)} %eq.10), kind=kLoop, calls=%fused_computation.5 | loop fusion | flops 393216 | bytes 1835009 | tf_op jit(solution)/shard_map/convert_element_type | solution.py:69
  36.8 2.6 %all-to-all-start.2 = ((bf16[32,8,512]{2,1,0:T(8,128)(2,1)}), bf16[32,8,512]{2,1,0:T(8,128)(2,1)S(1)}, u32[]{:S(2)}, u32[]{:S(2)}) async-start(bf16[32,8,512]{2,1,0:T(8,128)(2,1)} %bitcast.14), calls=%async_computation.2 | async-start | bytes 524288 | tf_op jit(solution)/shard_map/all_to_all | solution.py:70
  39.4 0.6 %fusion.4 = (f32[]{:T(128)}, f32[]{:T(128)}) fusion(f32[32]{0:T(128)S(1)} %get-tuple-element.11, s32[32]{0:T(128)S(1)} %copy-done.1, f32[32]{0:T(128)S(1)} %get-tuple-element.4), kind=kLoop, calls=%fused_computation.19 | loop fusion | flops 222 | bytes 392 | tf_op jit(solution)/shard_map/reduce_sum | solution.py:53
  41.3 2.1 %convolution_convert_fusion = bf16[128,8192]{1,0:T(8,128)(2,1)} fusion(bf16[32,8192]{1,0:T(8,128)(2,1)S(1)} %reshape.60, f32[32,128]{1,0:T(8,128)S(1)} %get-tuple-element.15, f32[32]{0:T(128)S(1)} %get-tuple-element.11, f32[32]{0:T(128)S(1)} %get-tuple-element.10, f32[32]{0:T(128)S(1)} %convert_element_type.23, s32[32]{0:T(128)S(1)} %broadcast_subtract_fusion), kind=kOutput, calls=%fused_computation | convolution fusion | flops 68186112 | bytes 2638336 | tf_op jit(solution)/shard_map/dot_general | solution.py:59
  43.4 6.5 %all-to-all-done.2 = bf16[32,8,512]{2,1,0:T(8,128)(2,1)S(1)} async-done(((bf16[32,8,512]{2,1,0:T(8,128)(2,1)}), bf16[32,8,512]{2,1,0:T(8,128)(2,1)S(1)}, u32[]{:S(2)}, u32[]{:S(2)}) %all-to-all-start.2) | async-done | bytes 262176 | tf_op jit(solution)/shard_map/all_to_all | solution.py:70
  50.0 0.7 %convert_reduce_fusion = f32[2,8,512]{2,1,0:T(8,128)} fusion(bf16[16,2,8,512]{3,2,1,0:T(8,128)(2,1)S(1)} %bitcast.46), kind=kLoop, calls=%fused_computation.6 | loop fusion | flops 253952 | bytes 294912 | tf_op jit(solution)/shard_map/reduce_sum | solution.py:71
  (4 shorter events, 0.1 us)
Async XLA Ops:
  0.6 21.2 %copy-start = (bf16[128,8192]{1,0:T(8,128)(2,1)S(1)}, bf16[128,8192]{1,0:T(8,128)(2,1)}, u32[]{:S(2)}) copy-start(bf16[128,8192]{1,0:T(8,128)(2,1)} %param.5) | copy-start | bytes 6291460
  19.2 1.5 %collective-permute-start = (bf16[32,8,512]{2,1,0:T(8,128)(2,1)S(1)}, bf16[32,8,512]{2,1,0:T(8,128)(2,1)S(1)}, u32[]{:S(2)}, u32[]{:S(2)}) collective-permute-start(bf16[32,8,512]{2,1,0:T(8,128)(2,1)S(1)} %all_to_all.15), channel_id=1, source_target_pairs={{0,1},{1,0},{2,3},{3,2},{4,5},{5,4},{6,7},{7,6},{8,9},{9,8},{10,11... | collective-permute-start | bytes 786440 | tf_op jit(solution)/shard_map/ppermute | solution.py:23
  21.4 4.8 %copy-start.1 = (s32[32]{0:T(128)S(1)}, s32[32]{0:T(128)}, u32[]{:S(2)}) copy-start(s32[32]{0:T(128)} %param.7) | copy-start | bytes 388
  23.7 9.7 %all-to-all-start.1 = ((f32[32,1,128]{2,1,0:T(1,128)}), f32[32,1,128]{2,1,0:T(1,128)S(1)}, u32[]{:S(2)}, u32[]{:S(2)}) async-start(f32[32,1,128]{2,1,0:T(1,128)} %broadcast_in_dim.10), calls=%async_computation.1 | async-start | bytes 32768 | tf_op jit(solution)/shard_map/all_to_all | solution.py:43
  34.0 2.0 %collective-permute-start.1 = (f32[4,8,8,512]{3,1,2,0:T(8,128)S(1)}, f32[4,8,8,512]{3,1,2,0:T(8,128)S(1)}, u32[]{:S(2)}, u32[]{:S(2)}) collective-permute-start(f32[4,8,8,512]{3,1,2,0:T(8,128)S(1)} %select_bitcast_fusion), channel_id=1, source_target_pairs={{0,1},{1,0},{2,3},{3,2},{4,5},{5,4},{6,7},{7,6},{8,9},{9,8},{10,11... | collective-permute-start | bytes 1572872 | tf_op jit(solution)/shard_map/ppermute | solution.py:68
  36.8 13.2 %all-to-all-start.2 = ((bf16[32,8,512]{2,1,0:T(8,128)(2,1)}), bf16[32,8,512]{2,1,0:T(8,128)(2,1)S(1)}, u32[]{:S(2)}, u32[]{:S(2)}) async-start(bf16[32,8,512]{2,1,0:T(8,128)(2,1)} %bitcast.14), calls=%async_computation.2 | async-start | bytes 524288 | tf_op jit(solution)/shard_map/all_to_all | solution.py:70

commit v2 on v1

v2 whole, which is shorter than its diff:
```python
import functools

import jax
import jax.numpy as jnp
from jax import lax
from jax.experimental import pallas as pl
from jax.experimental.pallas import tpu as pltpu
from jax.sharding import PartitionSpec as P

z_weight = 0.0001
BOTH = ("section", "tensor")
VMEM = pl.BlockSpec(memory_space=pltpu.VMEM)
SMEM = pl.BlockSpec(memory_space=pltpu.SMEM)


def logits_kernel(core_ref, rows_ref, own_ref, pair_ref, out_ref):
    sections, tensors, rows, half = rows_ref.shape
    core = core_ref[0]
    for which, weight_ref in enumerate((own_ref, pair_ref)):
        total = jnp.zeros(out_ref.shape[1:], jnp.float32)
        for t in range(tensors):
            x = rows_ref[:, t].reshape(sections * rows, half)
            start = pl.multiple_of(t * 2 * half + core * half, half)
            total += lax.dot_general(
                weight_ref[:, pl.ds(start, half)],
                x,
                (((1,), (1,)), ((), ())),
                preferred_element_type=jnp.float32,
            )
        out_ref[which] = total


def stats_kernel(first_ref, mine_ref, other_ref, targets_ref, logits_ref, stats_ref):
    own = mine_ref[0] + other_ref[1]
    pair = mine_ref[1] + other_ref[0]
    logits_ref[0] = own
    logits_ref[1] = pair
    ids = lax.broadcasted_iota(jnp.int32, own.shape, 0) + first_ref[0]
    top = jnp.max(own, axis=0, keepdims=True)
    total = jnp.sum(jnp.exp(own - top), axis=0, keepdims=True)
    picked = jnp.sum(jnp.where(ids == targets_ref[...], own, 0.0), axis=0, keepdims=True)
    parts = [top, total, picked]
    spare = stats_ref.shape[2] - 3 * top.shape[1]
    if spare:
        parts.append(jnp.zeros((1, spare), jnp.float32))
    row = jnp.concatenate(parts, axis=1)
    stats_ref[...] = jnp.broadcast_to(row[None], stats_ref.shape)


def grads_kernel(
    place_ref, logits_ref, log_total_ref, targets_ref, mask_ref, own_ref, pair_ref, dlogits_ref, out_ref
):
    sections, tensors, rows, half = out_ref.shape
    core = place_ref[0]
    log_total = log_total_ref[...]
    kept = mask_ref[...].astype(jnp.float32)
    factor = 1.0 + 2.0 * z_weight * log_total
    turned = []
    for which in range(2):
        probs = jnp.exp(logits_ref[which] - log_total)
        ids = lax.broadcasted_iota(jnp.int32, probs.shape, 0) + place_ref[1 + which]
        hit = (ids == targets_ref[...]).astype(jnp.float32)
        dlogits = kept * (factor * probs - hit)
        if which == 0:
            dlogits_ref[...] = dlogits.astype(jnp.bfloat16)
        turned.append(dlogits.T.astype(jnp.bfloat16))
    for t in range(tensors):
        start = pl.multiple_of(t * 2 * half + core * half, half)
        part = jnp.dot(turned[0], own_ref[:, pl.ds(start, half)], preferred_element_type=jnp.float32)
        part += jnp.dot(turned[1], pair_ref[:, pl.ds(start, half)], preferred_element_type=jnp.float32)
        out_ref[:, t] = part.reshape(sections, rows, half).astype(jnp.bfloat16)


def weight_kernel(core_ref, dlogits_ref, mine_ref, other_ref, out_ref):
    sections, _, rows, half = mine_ref.shape
    core = core_ref[0]
    for ref, place in ((mine_ref, core), (other_ref, 1 - core)):
        x = ref[:, 0].reshape(sections * rows, half)
        out_ref[:, pl.ds(pl.multiple_of(place * half, half), half)] = jnp.dot(
            dlogits_ref[...], x, preferred_element_type=jnp.float32
        ).astype(jnp.bfloat16)


def body(hidden, out_weight, targets, token_mask):
    sections, tensors = lax.axis_size("section"), lax.axis_size("tensor")
    devices = sections * tensors
    vocab_dev, width = out_weight.shape
    rows, block = hidden.shape
    half = block // 2
    tokens = sections * rows
    f32, bf16 = jnp.float32, jnp.bfloat16
    tensor = lax.axis_index("tensor")
    core = (tensor % 2).astype(jnp.int32)
    index = (lax.axis_index("section") * tensors + tensor).astype(jnp.int32)
    first = index * vocab_dev
    pair_first = first + (1 - 2 * core) * vocab_dev
    swap = [(i, i ^ 1) for i in range(tensors)]
    target_row = targets.reshape(1, tokens)
    mask_row = token_mask.reshape(1, tokens)

    pair_weight = lax.ppermute(out_weight, "tensor", swap)
    halves = hidden.reshape(rows, 2, half).transpose(1, 0, 2)
    sent = jnp.broadcast_to(halves[None], (devices // 2, 2, rows, half)).reshape(devices, rows, half)
    mine = lax.all_to_all(sent, BOTH, 0, 0).reshape(sections, tensors, rows, half)
    other = lax.ppermute(mine, "tensor", swap)

    flops = 2 * tokens * 2 * vocab_dev * width // 2
    partial = pl.pallas_call(
        logits_kernel,
        out_shape=jax.ShapeDtypeStruct((2, vocab_dev, tokens), f32),
        in_specs=[SMEM, VMEM, VMEM, VMEM],
        out_specs=VMEM,
        cost_estimate=pl.CostEstimate(flops=flops, bytes_accessed=2 * vocab_dev * width, transcendentals=0),
        name="half_logits",
    )(core[None], mine, out_weight, pair_weight)
    partial_other = lax.ppermute(partial, "tensor", swap)

    lanes = -(-3 * tokens // 128) * 128
    logits, stats = pl.pallas_call(
        stats_kernel,
        out_shape=(
            jax.ShapeDtypeStruct((2, vocab_dev, tokens), f32),
            jax.ShapeDtypeStruct((devices, 1, lanes), f32),
        ),
        in_specs=[SMEM, VMEM, VMEM, VMEM],
        out_specs=(VMEM, VMEM),
        cost_estimate=pl.CostEstimate(
            flops=8 * vocab_dev * tokens, bytes_accessed=24 * vocab_dev * tokens, transcendentals=vocab_dev * tokens
        ),
        name="row_stats",
    )(first[None], partial, partial_other, target_row)

    stats = lax.all_to_all(stats, BOTH, 0, 0).reshape(devices, lanes)
    tops = stats[:, :tokens]
    totals = stats[:, tokens : 2 * tokens]
    picked = jnp.sum(stats[:, 2 * tokens : 3 * tokens], axis=0)
    row_top = jnp.max(tops, axis=0)
    row_total = jnp.sum(totals * jnp.exp(tops - row_top[None, :]), axis=0)
    log_total = row_top + jnp.log(row_total)
    kept = token_mask.astype(f32)
    ce_loss = jnp.sum(kept * (log_total - picked)) / tokens
    z_loss = jnp.sum(kept * log_total * log_total) / tokens

    dlogits, parts = pl.pallas_call(
        grads_kernel,
        out_shape=(
            jax.ShapeDtypeStruct((vocab_dev, tokens), bf16),
            jax.ShapeDtypeStruct((sections, tensors, rows, half), bf16),
        ),
        in_specs=[SMEM, VMEM, VMEM, VMEM, VMEM, VMEM, VMEM],
        out_specs=(VMEM, VMEM),
        cost_estimate=pl.CostEstimate(
            flops=flops, bytes_accessed=2 * vocab_dev * width, transcendentals=2 * vocab_dev * tokens
        ),
        name="grad_parts",
    )(
        jnp.stack([core, first, pair_first]),
        logits,
        log_total.reshape(1, tokens),
        target_row,
        mask_row,
        out_weight,
        pair_weight,
    )
    shares = lax.all_to_all(parts.reshape(devices, rows, half), BOTH, 0, 0)

    grad_weight = pl.pallas_call(
        weight_kernel,
        out_shape=jax.ShapeDtypeStruct((vocab_dev, width), bf16),
        grid=(tensors,),
        in_specs=[
            SMEM,
            pl.BlockSpec((vocab_dev, tokens), lambda t: (0, 0)),
            pl.BlockSpec((sections, 1, rows, half), lambda t: (0, t, 0, 0)),
            pl.BlockSpec((sections, 1, rows, half), lambda t: (0, t, 0, 0)),
        ],
        out_specs=pl.BlockSpec((vocab_dev, block), lambda t: (0, t)),
        cost_estimate=pl.CostEstimate(
            flops=2 * tokens * vocab_dev * width,
            bytes_accessed=2 * vocab_dev * width + 2 * tokens * width,
            transcendentals=0,
        ),
        name="grad_weight",
    )(core[None], dlogits, mine, other)

    shares = shares.reshape(devices // 2, 2, rows, half)
    grad_hidden = jnp.sum(shares.astype(f32), axis=0).transpose(1, 0, 2).reshape(rows, block)
    return (ce_loss, z_loss, grad_hidden, grad_weight)


def solution(mesh):
    placed = (P("section", "tensor"), P(("section", "tensor"), None), P(), P())
    return jax.shard_map(
        body,
        mesh=mesh,
        in_specs=placed,
        out_specs=(P(), P(), P("section", "tensor"), P(("section", "tensor"), None)),
        check_vma=False,
    )
```

time: 53.3 us -> 60.6 us (1.14)
  blocking collectives: 17.7 us -> 0 us
  Pallas kernels: 0 us -> 14.5 us
  starting transfers between devices: 5.2 us -> 12.8 us
  waiting for transfers between devices: 16.4 us -> 21.5 us
  matrix products: 3.51 us -> 0 us
  local copies, waits for them, and re-layouts: 2.46 us -> 4.18 us
  other arithmetic: 3.31 us -> 2.52 us
    all_to_all x1 -> x0, blocking collectives: 17.7 us -> none  [body(): mine = lax.all_to_all(sent, BOTH, 0, 0)]
    pallas_call x0 -> x4, Pallas kernels: none -> 14.5 us  [the longest x1 5.55 us: body(): pl.pallas_call(weight_kernel, out_shape=jax.ShapeDtypeStruct((vocab_dev,...]
    all_to_all x2 -> x3, starting transfers between devices: 5.13 us -> 12.1 us  [the longest x1 6.95 us: body(): lax.all_to_all(sent, BOTH, 0, 0).reshape(sections, tensors, rows, half)]
    all_to_all x2 -> x3, waiting for transfers between devices: 13.6 us -> 19.8 us  [the longest x1 10.6 us: body(): lax.all_to_all(sent, BOTH, 0, 0).reshape(sections, tensors, rows, half)]
    dot_general x3 -> x0, matrix products: 3.51 us -> none  [the longest x1 2.13 us: body(): lax.dot_general(dlogits, gathered, (((0,), (0,)), ((), ())), preferred_el...]
    unnamed x4 -> x12, local copies, waits for them, and re-layouts: 0.02 us -> 2.73 us
    convert_element_type x2 -> x0, other arithmetic: 0.81 us -> none  [the longest x1 0.81 us: body(): pair.astype(jnp.bfloat16).transpose(0, 2, 1, 3).reshape(devices, rows, half)]
    ppermute x1, waiting for transfers between devices: 0.87 us -> 0.12 us  [body(): other = lax.ppermute(mine, 'tensor', swap)]
  transfers between devices with their start and end apart: 4 -> 6, of which waited for: 4 -> 5; matrix products, arithmetic and copies ran while one was open for 6% -> 3% of each run, Pallas kernels for 0% -> 9%
where the time goes in v2:
time: 60.6 us; the launch traced here: 59.7 us
  waiting for transfers between devices  21.5 us (35%)
  Pallas kernels  14.5 us (24%)
  starting transfers between devices  12.8 us (21%)
  between operations  4.26 us (7%)
  local copies, waits for them, and re-layouts  4.18 us (7%)
  other arithmetic  2.52 us (4%)
    all_to_all x1, waiting for transfers between devices, body(): lax.all_to_all(sent, BOTH, 0, 0).reshape(sections, tensors, rows, half)  10.6 us
    all_to_all x1, starting transfers between devices, body(): lax.all_to_all(sent, BOTH, 0, 0).reshape(sections, tensors, rows, half)  6.95 us
    all_to_all x1, waiting for transfers between devices, body(): stats = lax.all_to_all(stats, BOTH, 0, 0).reshape(devices, lanes)  6.51 us
    pallas_call x1, Pallas kernels, body(): pl.pallas_call(weight_kernel, out_shape=jax.ShapeDtypeStruct((vocab_dev,...  5.55 us
    pallas_call x1, Pallas kernels, body(): pl.pallas_call(logits_kernel, out_shape=jax.ShapeDtypeStruct((2, vocab_de...  3.65 us
    pallas_call x1, Pallas kernels, body(): pl.pallas_call(grads_kernel, out_shape=(jax.ShapeDtypeStruct((vocab_dev,...  3.55 us
    unnamed x12, local copies, waits for them, and re-layouts  2.73 us
    all_to_all x1, waiting for transfers between devices, body(): shares = lax.all_to_all(parts.reshape(devices, rows, half), BOTH, 0, 0)  2.72 us
  transfers between devices with their start and end apart: 6, of which 5 were waited for; matrix products, arithmetic and copies ran while one was open for 3% of the time, Pallas kernels for 9%

profile of v2, /device:TPU:0, one launch (start us, length us, event | category | flops | bytes accessed | tf_op | source)
XLA Modules:
  0.0 59.7 jit_solution(16322045102636685318)
XLA Ops:
  0.6 0.6 collective-permute-start
  1.2 1.4 %broadcast_in_dim.16 = bf16[16,2,8,512]{3,2,1,0:T(8,128)(2,1)} broadcast(bf16[2,8,512]{2,1,0:T(8,128)(2,1)} %bitcast.27), dimensions={1,2,3} | broadcast | bytes 278528 | tf_op jit(solution)/shard_map/broadcast_in_dim | solution.py:103
  2.6 6.9 %all-to-all-start = ((bf16[32,8,512]{2,1,0:T(8,128)(2,1)}), bf16[32,8,512]{2,1,0:T(8,128)(2,1)S(1)}, u32[]{:S(2)}, u32[]{:S(2)}) async-start(bf16[32,8,512]{2,1,0:T(8,128)(2,1)} %bitcast.4), calls=%async_computation | async-start | bytes 524288 | tf_op jit(solution)/shard_map/all_to_all | solution.py:104
  9.6 10.6 %all-to-all-done = bf16[32,8,512]{2,1,0:T(8,128)(2,1)S(1)} async-done(((bf16[32,8,512]{2,1,0:T(8,128)(2,1)}), bf16[32,8,512]{2,1,0:T(8,128)(2,1)S(1)}, u32[]{:S(2)}, u32[]{:S(2)}) %all-to-all-start) | async-done | bytes 262176 | tf_op jit(solution)/shard_map/all_to_all | solution.py:104
  20.2 0.0 copy-start.1
  20.2 0.0 collective-permute-done.pair_ref
  20.2 0.0 copy-start
  20.2 0.7 %copy-done.1 = bf16[32,8,512]{2,1,0:T(8,128)(2,1)} copy-done((bf16[32,8,512]{2,1,0:T(8,128)(2,1)}, bf16[32,8,512]{2,1,0:T(8,128)(2,1)S(1)}, u32[]{:S(2)}) %copy-start.1) | copy-done | bytes 262168
  20.8 0.7 %copy-done = bf16[128,8192]{1,0:T(8,128)(2,1)} copy-done((bf16[128,8192]{1,0:T(8,128)(2,1)}, bf16[128,8192]{1,0:T(8,128)(2,1)S(1)}, u32[]{:S(2)}) %copy-start) | copy-done | bytes 2097176
  21.6 0.0 copy-start.5
  21.6 3.6 %half_logits.1.mine_ref = f32[2,128,32]{2,1,0:T(8,128)} custom-call(s32[1]{0:T(128)} %bitcast.1.core_ref, bf16[4,8,8,512]{3,2,1,0:T(8,128)(2,1)} %bitcast.19, bf16[128,8192]{1,0:T(8,128)(2,1)} %own_ref.3, bf16[128,8192]{1,0:T(8,128)(2,1)} %copy-done), custom_call_target="tpu_custom_call" | custom-call | flops 67108864 | bytes 2097152 | tf_op jit(solution)/shard_map/half_logits/pallas_call | solution.py:108
  25.2 0.0 collective-permute-start.1
  25.2 1.6 %collective-permute-done.1.other_ref = f32[2,128,32]{2,1,0:T(8,128)S(1)} collective-permute-done((f32[2,128,32]{2,1,0:T(8,128)}, f32[2,128,32]{2,1,0:T(8,128)S(1)}, u32[]{:S(2)}, u32[]{:S(2)}) %collective-permute-start.1) | collective-permute-done | bytes 32800 | tf_op jit(solution)/shard_map/ppermute | solution.py:116
  26.8 0.0 copy-start.4
  26.8 0.6 %copy-done.4 = f32[2,128,32]{2,1,0:T(8,128)} copy-done((f32[2,128,32]{2,1,0:T(8,128)}, f32[2,128,32]{2,1,0:T(8,128)S(1)}, u32[]{:S(2)}) %copy-start.4) | copy-done | bytes 32792
  27.4 1.7 %row_stats.1 = (f32[2,128,32]{2,1,0:T(8,128)}, f32[32,1,128]{2,1,0:T(1,128)}) custom-call(s32[1]{0:T(128)} %bitcast.first_ref, f32[2,128,32]{2,1,0:T(8,128)} %half_logits.1.mine_ref, f32[2,128,32]{2,1,0:T(8,128)} %copy-done.4, s32[1,32]{1,0:T(1,128)} %bitcast.28), custom_call_target="tpu_custom_call" | custom-call | flops 32768 | bytes 98304 | tf_op jit(solution)/shard_map/row_stats/pallas_call | solution.py:119
  29.1 2.5 %all-to-all-start.1 = ((f32[32,1,128]{2,1,0:T(1,128)}), f32[32,1,128]{2,1,0:T(1,128)S(1)}, u32[]{:S(2)}, u32[]{:S(2)}) async-start(f32[32,1,128]{2,1,0:T(1,128)} %get-tuple-element.8), calls=%async_computation.1 | async-start | bytes 32768 | tf_op jit(solution)/shard_map/all_to_all | solution.py:133
  31.7 0.6 pad_add_fusion.place_ref
  32.3 6.5 %all-to-all-done.1 = f32[32,1,128]{2,1,0:T(1,128)S(1)} async-done(((f32[32,1,128]{2,1,0:T(1,128)}), f32[32,1,128]{2,1,0:T(1,128)S(1)}, u32[]{:S(2)}, u32[]{:S(2)}) %all-to-all-start.1) | async-done | bytes 16416 | tf_op jit(solution)/shard_map/all_to_all | solution.py:133
  38.8 0.1 fusion
  38.9 0.0 copy-done.5
  38.9 1.1 %fusion.1 = (f32[]{:T(128)}, f32[]{:T(128)}, f32[1,32]{1,0:T(1,128)}) fusion(s32[32]{0:T(128)S(1)} %copy-done.5, f32[32]{0:T(128)S(1)} %slice_reduce_fusion.1, f32[32]{0:T(128)S(1)} %get-tuple-element.12, f32[32]{0:T(128)S(1)} %get-tuple-element.13), kind=kLoop, calls=%fused_computation.6 | loop fusion | flops 254 | bytes 648 | tf_op jit(solution)/shard_map/reduce_sum | solution.py:142
  40.1 0.0 copy-start.2
  40.1 3.6 %grad_parts.1 = (bf16[128,32]{1,0:T(8,128)(2,1)}, bf16[4,8,8,512]{3,2,1,0:T(8,128)(2,1)}) custom-call(s32[3]{0:T(128)} %pad_add_fusion.place_ref, f32[2,128,32]{2,1,0:T(8,128)} %get-tuple-element.9.logits_ref, f32[1,32]{1,0:T(1,128)} %get-tuple-element.16.log_total_ref, s32[1,32]{1,0:T(1,128)} %bitcast.29, s32[1,32]{1,0:T(1,128)} %bitcast.30, ...), custom_call_target="tpu_custom_call" | custom-call | flops 67108864 | bytes 2097152 | tf_op jit(solution)/shard_map/grad_parts/pallas_call | solution.py:144
  43.6 2.6 %all-to-all-start.2 = ((bf16[32,8,512]{2,1,0:T(8,128)(2,1)}), bf16[32,8,512]{2,1,0:T(8,128)(2,1)S(1)}, u32[]{:S(2)}, u32[]{:S(2)}) async-start(bf16[32,8,512]{2,1,0:T(8,128)(2,1)} %bitcast.25), calls=%async_computation.2 | async-start | bytes 524288 | tf_op jit(solution)/shard_map/all_to_all | solution.py:165
  46.2 0.0 copy-done.2
  46.2 0.2 collective-permute-start.2
  47.7 0.1 collective-permute-done.2.other_ref
  47.8 0.0 copy-start.3
  47.8 0.7 %copy-done.3 = bf16[4,8,8,512]{3,2,1,0:T(8,128)(2,1)} copy-done((bf16[4,8,8,512]{3,2,1,0:T(8,128)(2,1)}, bf16[4,8,8,512]{3,2,1,0:T(8,128)(2,1)S(1)}, u32[]{:S(2)}) %copy-start.3) | copy-done | bytes 262168
  48.5 5.6 %grad_weight.1 = bf16[128,8192]{1,0:T(8,128)(2,1)} custom-call(s32[1]{0:T(128)} %bitcast.1.core_ref, bf16[128,32]{1,0:T(8,128)(2,1)} %get-tuple-element.11.dlogits_ref, bf16[4,8,8,512]{3,2,1,0:T(8,128)(2,1)} %bitcast.20, bf16[4,8,8,512]{3,2,1,0:T(8,128)(2,1)} %copy-done.3), custom_call_target="tpu_custom_call" | custom-call | flops 67108864 | bytes 2621440 | tf_op jit(solution)/shard_map/grad_weight/pallas_call | solution.py:167
  54.1 2.7 %all-to-all-done.2 = bf16[32,8,512]{2,1,0:T(8,128)(2,1)S(1)} async-done(((bf16[32,8,512]{2,1,0:T(8,128)(2,1)}), bf16[32,8,512]{2,1,0:T(8,128)(2,1)S(1)}, u32[]{:S(2)}, u32[]{:S(2)}) %all-to-all-start.2) | async-done | bytes 262176 | tf_op jit(solution)/shard_map/all_to_all | solution.py:165
  56.8 0.7 %convert_reduce_fusion = f32[2,8,512]{2,1,0:T(8,128)} fusion(bf16[16,2,8,512]{3,2,1,0:T(8,128)(2,1)S(1)} %bitcast.22), kind=kLoop, calls=%fused_computation | loop fusion | flops 253952 | bytes 294912 | tf_op jit(solution)/shard_map/reduce_sum | solution.py:187
  (1 shorter events, 0.0 us)
Async XLA Ops:
  0.6 19.5 %collective-permute-start = (bf16[128,8192]{1,0:T(8,128)(2,1)}, bf16[128,8192]{1,0:T(8,128)(2,1)S(1)}, u32[]{:S(2)}, u32[]{:S(2)}) collective-permute-start(bf16[128,8192]{1,0:T(8,128)(2,1)} %own_ref.3), channel_id=1, source_target_pairs={{0,1},{1,0},{2,3},{3,2},{4,5},{5,4},{6,7},{7,6},{8,9},{9,8},{10,11... | collective-permute-start | bytes 6291464 | tf_op jit(solution)/shard_map/ppermute | solution.py:101
  2.6 17.5 %all-to-all-start = ((bf16[32,8,512]{2,1,0:T(8,128)(2,1)}), bf16[32,8,512]{2,1,0:T(8,128)(2,1)S(1)}, u32[]{:S(2)}, u32[]{:S(2)}) async-start(bf16[32,8,512]{2,1,0:T(8,128)(2,1)} %bitcast.4), calls=%async_computation | async-start | bytes 524288 | tf_op jit(solution)/shard_map/all_to_all | solution.py:104
  20.2 0.7 %copy-start.1 = (bf16[32,8,512]{2,1,0:T(8,128)(2,1)}, bf16[32,8,512]{2,1,0:T(8,128)(2,1)S(1)}, u32[]{:S(2)}) copy-start(bf16[32,8,512]{2,1,0:T(8,128)(2,1)S(1)} %all-to-all-done) | copy-start | bytes 786436
  20.2 1.4 %copy-start = (bf16[128,8192]{1,0:T(8,128)(2,1)}, bf16[128,8192]{1,0:T(8,128)(2,1)S(1)}, u32[]{:S(2)}) copy-start(bf16[128,8192]{1,0:T(8,128)(2,1)S(1)} %collective-permute-done.pair_ref) | copy-start | bytes 6291460
  21.6 17.3 %copy-start.5 = (s32[32]{0:T(128)S(1)}, s32[32]{0:T(128)}, u32[]{:S(2)}) copy-start(s32[32]{0:T(128)} %param.7) | copy-start | bytes 388
  25.2 1.6 %collective-permute-start.1 = (f32[2,128,32]{2,1,0:T(8,128)}, f32[2,128,32]{2,1,0:T(8,128)S(1)}, u32[]{:S(2)}, u32[]{:S(2)}) collective-permute-start(f32[2,128,32]{2,1,0:T(8,128)} %half_logits.1.mine_ref), channel_id=1, source_target_pairs={{0,1},{1,0},{2,3},{3,2},{4,5},{5,4},{6,7},{7,6},{8,9},{9,8},{10,11... | collective-permute-start | bytes 98312 | tf_op jit(solution)/shard_map/ppermute | solution.py:116
  26.8 0.6 %copy-start.4 = (f32[2,128,32]{2,1,0:T(8,128)}, f32[2,128,32]{2,1,0:T(8,128)S(1)}, u32[]{:S(2)}) copy-start(f32[2,128,32]{2,1,0:T(8,128)S(1)} %collective-permute-done.1.other_ref) | copy-start | bytes 98308
  29.1 9.7 %all-to-all-start.1 = ((f32[32,1,128]{2,1,0:T(1,128)}), f32[32,1,128]{2,1,0:T(1,128)S(1)}, u32[]{:S(2)}, u32[]{:S(2)}) async-start(f32[32,1,128]{2,1,0:T(1,128)} %get-tuple-element.8), calls=%async_computation.1 | async-start | bytes 32768 | tf_op jit(solution)/shard_map/all_to_all | solution.py:133
  40.1 6.1 %copy-start.2 = (bf16[32,8,512]{2,1,0:T(8,128)(2,1)S(1)}, bf16[32,8,512]{2,1,0:T(8,128)(2,1)}, u32[]{:S(2)}) copy-start(bf16[32,8,512]{2,1,0:T(8,128)(2,1)} %copy-done.1) | copy-start | bytes 786436
  43.6 13.2 %all-to-all-start.2 = ((bf16[32,8,512]{2,1,0:T(8,128)(2,1)}), bf16[32,8,512]{2,1,0:T(8,128)(2,1)S(1)}, u32[]{:S(2)}, u32[]{:S(2)}) async-start(bf16[32,8,512]{2,1,0:T(8,128)(2,1)} %bitcast.25), calls=%async_computation.2 | async-start | bytes 524288 | tf_op jit(solution)/shard_map/all_to_all | solution.py:165
  46.2 1.6 %collective-permute-start.2 = (bf16[4,8,8,512]{3,2,1,0:T(8,128)(2,1)S(1)}, bf16[4,8,8,512]{3,2,1,0:T(8,128)(2,1)S(1)}, u32[]{:S(2)}, u32[]{:S(2)}) collective-permute-start(bf16[4,8,8,512]{3,2,1,0:T(8,128)(2,1)S(1)} %bitcast.21), channel_id=1, source_target_pairs={{0,1},{1,0},{2,3},{3,2},{4,5},{5,4},{6,7},{7,6},{8,9},{9,8},{10,11... | collective-permute-start | bytes 786440 | tf_op jit(solution)/shard_map/ppermute | solution.py:105
  47.8 0.7 %copy-start.3 = (bf16[4,8,8,512]{3,2,1,0:T(8,128)(2,1)}, bf16[4,8,8,512]{3,2,1,0:T(8,128)(2,1)S(1)}, u32[]{:S(2)}) copy-start(bf16[4,8,8,512]{3,2,1,0:T(8,128)(2,1)S(1)} %collective-permute-done.2.other_ref) | copy-start | bytes 786436

commit v3 on v2

v3 whole, which is shorter than its diff:
```python
import functools

import jax
import jax.numpy as jnp
from jax import lax
from jax.experimental import pallas as pl
from jax.experimental.pallas import tpu as pltpu
from jax.sharding import PartitionSpec as P


z_weight = 0.0001
BOTH = ("section", "tensor")
VMEM = pl.BlockSpec(memory_space=pltpu.VMEM)
SMEM = pl.BlockSpec(memory_space=pltpu.SMEM)
SMALL = pltpu.CompilerParams(vmem_limit_bytes=16 << 20)


def split_kernel(half, place_ref, weight_ref, keep_ref, give_ref):
    core = place_ref[0]
    for t in range(keep_ref.shape[1] // half):
        for ref, place in ((keep_ref, core), (give_ref, 1 - core)):
            start = pl.multiple_of((2 * t + place) * half, half)
            ref[:, t * half : (t + 1) * half] = weight_ref[:, pl.ds(start, half)]


def logits_kernel(rows_ref, own_ref, pair_ref, out_ref):
    sections, tensors, rows, half = rows_ref.shape
    for which, weight_ref in enumerate((own_ref, pair_ref)):
        total = jnp.zeros(out_ref.shape[1:], jnp.float32)
        for t in range(tensors):
            x = rows_ref[:, t].reshape(sections * rows, half)
            total += lax.dot_general(
                weight_ref[:, t * half : (t + 1) * half],
                x,
                (((1,), (1,)), ((), ())),
                preferred_element_type=jnp.float32,
            )
        out_ref[which] = total


def stats_kernel(place_ref, mine_ref, other_ref, targets_ref, logits_ref, stats_ref):
    own = mine_ref[0] + other_ref[1]
    pair = mine_ref[1] + other_ref[0]
    logits_ref[0] = own
    logits_ref[1] = pair
    ids = lax.broadcasted_iota(jnp.int32, own.shape, 0) + place_ref[1]
    top = jnp.max(own, axis=0, keepdims=True)
    total = jnp.sum(jnp.exp(own - top), axis=0, keepdims=True)
    picked = jnp.sum(jnp.where(ids == targets_ref[...], own, 0.0), axis=0, keepdims=True)
    parts = [top, total, picked]
    spare = stats_ref.shape[2] - 3 * top.shape[1]
    if spare:
        parts.append(jnp.zeros((1, spare), jnp.float32))
    row = jnp.concatenate(parts, axis=1)
    stats_ref[...] = jnp.broadcast_to(row[None], stats_ref.shape)


def grads_kernel(
    place_ref, logits_ref, log_total_ref, targets_ref, mask_ref, own_ref, pair_ref, dlogits_ref, out_ref, kept_ref
):
    sections, tensors, rows, half = out_ref.shape
    log_total = log_total_ref[...]
    kept_ref[...] = log_total
    kept = mask_ref[...].astype(jnp.float32)
    factor = 1.0 + 2.0 * z_weight * log_total
    turned = []
    for which in range(2):
        probs = jnp.exp(logits_ref[which] - log_total)
        ids = lax.broadcasted_iota(jnp.int32, probs.shape, 0) + place_ref[1 + which]
        hit = (ids == targets_ref[...]).astype(jnp.float32)
        dlogits = kept * (factor * probs - hit)
        if which == 0:
            dlogits_ref[...] = dlogits.astype(jnp.bfloat16)
        turned.append(dlogits.T.astype(jnp.bfloat16))
    for t in range(tensors):
        columns = slice(t * half, (t + 1) * half)
        part = jnp.dot(turned[0], own_ref[:, columns], preferred_element_type=jnp.float32)
        part += jnp.dot(turned[1], pair_ref[:, columns], preferred_element_type=jnp.float32)
        out_ref[:, t] = part.reshape(sections, rows, half).astype(jnp.bfloat16)


def weight_kernel(place_ref, dlogits_ref, mine_ref, other_ref, out_ref):
    sections, _, rows, half = mine_ref.shape
    core = place_ref[0]
    for ref, place in ((mine_ref, core), (other_ref, 1 - core)):
        x = ref[:, 0].reshape(sections * rows, half)
        out_ref[:, pl.ds(pl.multiple_of(place * half, half), half)] = jnp.dot(
            dlogits_ref[...], x, preferred_element_type=jnp.float32
        ).astype(jnp.bfloat16)


def body(hidden, out_weight, targets, token_mask):
    sections, tensors = lax.axis_size("section"), lax.axis_size("tensor")
    devices = sections * tensors
    vocab_dev, width = out_weight.shape
    rows, block = hidden.shape
    half = block // 2
    tokens = sections * rows
    f32, bf16 = jnp.float32, jnp.bfloat16
    tensor = lax.axis_index("tensor")
    core = (tensor % 2).astype(jnp.int32)
    first = (lax.axis_index("section") * tensors + tensor).astype(jnp.int32) * vocab_dev
    place = jnp.stack([core, first, first + (1 - 2 * core) * vocab_dev])
    swap = [(i, i ^ 1) for i in range(tensors)]
    target_row = targets.reshape(1, tokens)
    mask_row = token_mask.reshape(1, tokens)

    halves = hidden.reshape(rows, 2, half).transpose(1, 0, 2)
    sent = jnp.broadcast_to(halves[None], (devices // 2, 2, rows, half)).reshape(devices, rows, half)
    mine = lax.all_to_all(sent, BOTH, 0, 0)
    mine = mine.reshape(sections, tensors, rows, half)
    other = lax.ppermute(mine, "tensor", swap)

    half_weight = jax.ShapeDtypeStruct((vocab_dev, width // 2), bf16)
    own_weight, given = pl.pallas_call(
        functools.partial(split_kernel, half),
        out_shape=(half_weight, half_weight),
        in_specs=[SMEM, VMEM],
        out_specs=(VMEM, VMEM),
        compiler_params=SMALL,
        cost_estimate=pl.CostEstimate(flops=0, bytes_accessed=4 * vocab_dev * width, transcendentals=0),
        name="split_weight",
    )(place, out_weight)
    pair_weight = lax.ppermute(given, "tensor", swap)

    flops = 2 * tokens * vocab_dev * width
    partial = pl.pallas_call(
        logits_kernel,
        out_shape=jax.ShapeDtypeStruct((2, vocab_dev, tokens), f32),
        in_specs=[VMEM, VMEM, VMEM],
        out_specs=VMEM,
        compiler_params=SMALL,
        cost_estimate=pl.CostEstimate(flops=flops, bytes_accessed=2 * vocab_dev * width, transcendentals=0),
        name="half_logits",
    )(mine, own_weight, pair_weight)
    partial_other = lax.ppermute(partial, "tensor", swap)

    lanes = -(-3 * tokens // 128) * 128
    logits, stats = pl.pallas_call(
        stats_kernel,
        out_shape=(
            jax.ShapeDtypeStruct((2, vocab_dev, tokens), f32),
            jax.ShapeDtypeStruct((devices, 1, lanes), f32),
        ),
        in_specs=[SMEM, VMEM, VMEM, VMEM],
        out_specs=(VMEM, VMEM),
        compiler_params=SMALL,
        cost_estimate=pl.CostEstimate(
            flops=8 * vocab_dev * tokens, bytes_accessed=24 * vocab_dev * tokens, transcendentals=vocab_dev * tokens
        ),
        name="row_stats",
    )(place, partial, partial_other, target_row)

    stats = lax.all_to_all(stats, BOTH, 0, 0).reshape(devices, lanes)
    tops = stats[:, :tokens]
    totals = stats[:, tokens : 2 * tokens]
    row_top = jnp.max(tops, axis=0)
    row_total = jnp.sum(totals * jnp.exp(tops - row_top[None, :]), axis=0)
    log_total = row_top + jnp.log(row_total)

    dlogits, parts, log_total = pl.pallas_call(
        grads_kernel,
        out_shape=(
            jax.ShapeDtypeStruct((vocab_dev, tokens), bf16),
            jax.ShapeDtypeStruct((sections, tensors, rows, half), bf16),
            jax.ShapeDtypeStruct((1, tokens), f32),
        ),
        in_specs=[SMEM, VMEM, VMEM, VMEM, VMEM, VMEM, VMEM],
        out_specs=(VMEM, VMEM, VMEM),
        compiler_params=SMALL,
        cost_estimate=pl.CostEstimate(
            flops=flops, bytes_accessed=2 * vocab_dev * width, transcendentals=2 * vocab_dev * tokens
        ),
        name="grad_parts",
    )(place, logits, log_total.reshape(1, tokens), target_row, mask_row, own_weight, pair_weight)
    shares = lax.all_to_all(parts.reshape(devices, rows, half), BOTH, 0, 0)

    log_total = log_total.reshape(tokens)
    picked = jnp.sum(stats[:, 2 * tokens : 3 * tokens], axis=0)
    kept = token_mask.astype(f32)
    ce_loss = jnp.sum(kept * (log_total - picked)) / tokens
    z_loss = jnp.sum(kept * log_total * log_total) / tokens

    grad_weight = pl.pallas_call(
        weight_kernel,
        out_shape=jax.ShapeDtypeStruct((vocab_dev, width), bf16),
        grid=(tensors,),
        in_specs=[
            SMEM,
            pl.BlockSpec((vocab_dev, tokens), lambda t: (0, 0)),
            pl.BlockSpec((sections, 1, rows, half), lambda t: (0, t, 0, 0)),
            pl.BlockSpec((sections, 1, rows, half), lambda t: (0, t, 0, 0)),
        ],
        out_specs=pl.BlockSpec((vocab_dev, block), lambda t: (0, t)),
        compiler_params=SMALL,
        cost_estimate=pl.CostEstimate(
            flops=flops, bytes_accessed=2 * vocab_dev * width + 2 * tokens * width, transcendentals=0
        ),
        name="grad_weight",
    )(place, dlogits, mine, other)

    shares = shares.reshape(devices // 2, 2, rows, half)
    grad_hidden = jnp.sum(shares.astype(f32), axis=0).transpose(1, 0, 2).reshape(rows, block)
    return (ce_loss, z_loss, grad_hidden, grad_weight)


def solution(mesh):
    placed = (P("section", "tensor"), P(("section", "tensor"), None), P(), P())
    return jax.shard_map(
        body,
        mesh=mesh,
        in_specs=placed,
        out_specs=(P(), P(), P("section", "tensor"), P(("section", "tensor"), None)),
        check_vma=False,
    )
```

time: 60.6 us -> 51.3 us (0.85); the launches traced: 59.7 us -> 51.1 us
  blocking collectives: 0 us -> 26.7 us
  waiting for transfers between devices: 21.5 us -> 5.37 us
  starting transfers between devices: 12.8 us -> 3.4 us
  Pallas kernels: 14.5 us -> 8.19 us
  local copies, waits for them, and re-layouts: 4.18 us -> 1.63 us
  other arithmetic: 2.52 us -> 1.46 us
    all_to_all x0 -> x2, blocking collectives: none -> 26.7 us  [the longest x1 17.3 us: body(): mine = lax.all_to_all(sent, BOTH, 0, 0)]
    all_to_all x2 -> x0, waiting for transfers between devices: 17.1 us -> none  [the longest x1 10.6 us: body(): lax.all_to_all(sent, BOTH, 0, 0).reshape(sections, tensors, rows, half)]
    all_to_all x2 -> x0, starting transfers between devices: 9.49 us -> none  [the longest x1 6.95 us: body(): lax.all_to_all(sent, BOTH, 0, 0).reshape(sections, tensors, rows, half)]
    pallas_call x1, Pallas kernels: 3.65 us -> 0.67 us  [body(): pl.pallas_call(logits_kernel, out_shape=jax.ShapeDtypeStruct((2, vocab_de...]
    pallas_call x1, Pallas kernels: 3.55 us -> 1.72 us  [body(): pl.pallas_call(grads_kernel, out_shape=(jax.ShapeDtypeStruct((vocab_dev,...]
    broadcast_in_dim x1, local copies, waits for them, and re-layouts: 1.44 us -> 0.02 us  [body(): jnp.broadcast_to(halves[None], (devices // 2, 2, rows, half))]
    all_to_all x1, waiting for transfers between devices: 2.72 us -> 4.03 us  [body(): shares = lax.all_to_all(parts.reshape(devices, rows, half), BOTH, 0, 0)]
    unnamed x12 -> x8, local copies, waits for them, and re-layouts: 2.73 us -> 1.61 us
  transfers between devices with their start and end apart: 6 -> 4, of which waited for: 5 -> 2; matrix products, arithmetic and copies ran while one was open for 3% -> 1% of each run, Pallas kernels for 9% -> 9%
where the time goes in v3:
time: 51.3 us; the launch traced here: 51.1 us
  blocking collectives  26.7 us (52%)
  Pallas kernels  8.19 us (16%)
  waiting for transfers between devices  5.37 us (10%)
  between operations  4.3 us (8%)
  starting transfers between devices  3.4 us (7%)
  local copies, waits for them, and re-layouts  1.63 us (3%)
  other arithmetic  1.46 us (3%)
    all_to_all x1, blocking collectives, body(): mine = lax.all_to_all(sent, BOTH, 0, 0)  17.3 us
    all_to_all x1, blocking collectives, body(): stats = lax.all_to_all(stats, BOTH, 0, 0).reshape(devices, lanes)  9.38 us
    pallas_call x1, Pallas kernels, body(): pl.pallas_call(weight_kernel, out_shape=jax.ShapeDtypeStruct((vocab_dev,...  4.45 us
    all_to_all x1, waiting for transfers between devices, body(): shares = lax.all_to_all(parts.reshape(devices, rows, half), BOTH, 0, 0)  4.03 us
    all_to_all x1, starting transfers between devices, body(): shares = lax.all_to_all(parts.reshape(devices, rows, half), BOTH, 0, 0)  2.58 us
    pallas_call x1, Pallas kernels, body(): pl.pallas_call(grads_kernel, out_shape=(jax.ShapeDtypeStruct((vocab_dev,...  1.72 us
    unnamed x8, local copies, waits for them, and re-layouts  1.61 us
    ppermute x1, waiting for transfers between devices, body(): partial_other = lax.ppermute(partial, 'tensor', swap)  1.33 us
  transfers between devices with their start and end apart: 4, of which 2 were waited for; matrix products, arithmetic and copies ran while one was open for 1% of the time, Pallas kernels for 9%

profile of v3, /device:TPU:0, one launch (start us, length us, event | category | flops | bytes accessed | tf_op | source)
XLA Modules:
  0.0 51.1 jit_solution(17194630949396394081)
XLA Ops:
  0.6 0.0 copy-start.3
  0.7 0.1 pad_add_fusion.place_ref
  0.7 0.0 copy-start
  0.7 1.6 %copy-done = bf16[128,8192]{1,0:T(8,128)(2,1)S(1)} copy-done((bf16[128,8192]{1,0:T(8,128)(2,1)S(1)}, bf16[128,8192]{1,0:T(8,128)(2,1)}, u32[]{:S(2)}) %copy-start) | copy-done | bytes 2097176
  2.3 0.7 %split_weight.1 = (bf16[128,4096]{1,0:T(8,128)(2,1)S(1)}, bf16[128,4096]{1,0:T(8,128)(2,1)S(1)}) custom-call(s32[3]{0:T(128)S(1)} %pad_add_fusion.place_ref, bf16[128,8192]{1,0:T(8,128)(2,1)S(1)} %copy-done), custom_call_target="tpu_custom_call" | custom-call | bytes 4194304 | tf_op jit(solution)/shard_map/split_weight/pallas_call | solution.py:115
  3.0 0.0 copy-start.1
  3.0 0.0 copy-start.2
  3.0 0.6 %collective-permute-start = (bf16[128,4096]{1,0:T(8,128)(2,1)S(1)}, bf16[128,4096]{1,0:T(8,128)(2,1)S(1)}, u32[]{:S(2)}, u32[]{:S(2)}) collective-permute-start(bf16[128,4096]{1,0:T(8,128)(2,1)S(1)} %get-tuple-element.12), channel_id=1, source_target_pairs={{0,1},{1,0},{2,3},{3,2},{4,5},{5,4},{6,7},{7,6},{8,9},{9,8},{10,11... | collective-permute-start | bytes 3145736 | tf_op jit(solution)/shard_map/ppermute | solution.py:124
  3.6 0.0 copy-done.3
  3.6 17.3 %all_to_all.15 = bf16[32,8,512]{2,1,0:T(8,128)(2,1)S(1)} all-to-all(bf16[32,8,512]{2,1,0:T(8,128)(2,1)S(1)} %bitcast.33), channel_id=1, replica_groups=mesh['section'=4,'tensor'=8] {'section','tensor'}, dimensions={0} | all-to-all | bytes 524288 | tf_op jit(solution)/shard_map/all_to_all | solution.py:110
  21.0 0.0 collective-permute-done.pair_ref
  21.0 0.7 %half_logits.1.mine_ref = f32[2,128,32]{2,1,0:T(8,128)S(1)} custom-call(bf16[4,8,8,512]{3,2,1,0:T(8,128)(2,1)S(1)} %bitcast.26, bf16[128,4096]{1,0:T(8,128)(2,1)S(1)} %get-tuple-element.11.own_ref, bf16[128,4096]{1,0:T(8,128)(2,1)S(1)} %collective-permute-done.pair_ref), custom_call_target="tpu_custom_call" | custom-call | flops 67108864 | bytes 2097152 | tf_op jit(solution)/shard_map/half_logits/pallas_call | solution.py:127
  21.6 0.1 collective-permute-start.1
  21.7 1.3 %collective-permute-done.1.other_ref = f32[2,128,32]{2,1,0:T(8,128)S(1)} collective-permute-done((f32[2,128,32]{2,1,0:T(8,128)S(1)}, f32[2,128,32]{2,1,0:T(8,128)S(1)}, u32[]{:S(2)}, u32[]{:S(2)}) %collective-permute-start.1) | collective-permute-done | bytes 32800 | tf_op jit(solution)/shard_map/ppermute | solution.py:136
  23.1 0.0 copy-done.1
  23.1 0.7 %row_stats.1 = (f32[2,128,32]{2,1,0:T(8,128)S(1)}, f32[32,1,128]{2,1,0:T(1,128)S(1)}) custom-call(s32[3]{0:T(128)S(1)} %pad_add_fusion.place_ref, f32[2,128,32]{2,1,0:T(8,128)S(1)} %half_logits.1.mine_ref, f32[2,128,32]{2,1,0:T(8,128)S(1)} %collective-permute-done.1.other_ref, s32[1,32]{1,0:T(1,128)S(1)} %bitcast.29), custom_call_target="tpu_custom_call" | custom-call | flops 32768 | bytes 98304 | tf_op jit(solution)/shard_map/row_stats/pallas_call | solution.py:139
  23.7 9.4 %all_to_all.16 = f32[32,1,128]{2,1,0:T(1,128)S(1)} all-to-all(f32[32,1,128]{2,1,0:T(1,128)S(1)} %get-tuple-element.14), channel_id=1, replica_groups=mesh['section'=4,'tensor'=8] {'section','tensor'}, dimensions={0} | all-to-all | bytes 32768 | tf_op jit(solution)/shard_map/all_to_all | solution.py:154
  33.1 0.1 fusion
  33.2 0.0 copy-done.2
  33.3 1.7 %grad_parts.1 = (bf16[128,32]{1,0:T(8,128)(2,1)S(1)}, bf16[4,8,8,512]{3,2,1,0:T(8,128)(2,1)}, f32[1,32]{1,0:T(1,128)S(1)}) custom-call(s32[3]{0:T(128)S(1)} %pad_add_fusion.place_ref, f32[2,128,32]{2,1,0:T(8,128)S(1)} %get-tuple-element.13.logits_ref, f32[1,32]{1,0:T(1,128)S(1)} %add_bitcast_fusion.log_total_ref, s32[1,32]{1,0:T(1,128)S(1)} %bitcast.30, ...), custom_call_target="tpu_custom_call" | custom-call | flops 67108864 | bytes 2097152 | tf_op jit(solution)/shard_map/grad_parts/pallas_call | solution.py:161
  35.0 2.6 %all-to-all-start.2 = ((bf16[32,8,512]{2,1,0:T(8,128)(2,1)}), bf16[32,8,512]{2,1,0:T(8,128)(2,1)S(1)}, u32[]{:S(2)}, u32[]{:S(2)}) async-start(bf16[32,8,512]{2,1,0:T(8,128)(2,1)} %bitcast.12), calls=%async_computation.2 | async-start | bytes 524288 | tf_op jit(solution)/shard_map/all_to_all | solution.py:176
  37.6 0.2 collective-permute-start.2
  37.7 0.6 %fusion.1 = (f32[]{:T(128)}, f32[]{:T(128)}) fusion(f32[1,32]{1,0:T(1,128)S(1)} %get-tuple-element.15, s32[32]{0:T(128)S(1)} %copy-done.2, f32[32]{0:T(128)S(1)} %get-tuple-element.19), kind=kLoop, calls=%fused_computation.6 | loop fusion | flops 222 | bytes 392 | tf_op jit(solution)/shard_map/reduce_sum | solution.py:182
  39.6 0.0 collective-permute-done.2.other_ref
  39.7 4.4 %grad_weight.1 = bf16[128,8192]{1,0:T(8,128)(2,1)} custom-call(s32[3]{0:T(128)S(1)} %pad_add_fusion.place_ref, bf16[128,32]{1,0:T(8,128)(2,1)S(1)} %get-tuple-element.17.dlogits_ref, bf16[4,8,8,512]{3,2,1,0:T(8,128)(2,1)S(1)} %bitcast.28, bf16[4,8,8,512]{3,2,1,0:T(8,128)(2,1)S(1)} %collective-permute-done.2.other_ref), custom_call_target="tpu_custom_call" | custom-call | flops 67108864 | bytes 2621440 | tf_op jit(solution)/shard_map/grad_weight/pallas_call | solution.py:184
  44.1 4.0 %all-to-all-done.2 = bf16[32,8,512]{2,1,0:T(8,128)(2,1)S(1)} async-done(((bf16[32,8,512]{2,1,0:T(8,128)(2,1)}), bf16[32,8,512]{2,1,0:T(8,128)(2,1)S(1)}, u32[]{:S(2)}, u32[]{:S(2)}) %all-to-all-start.2) | async-done | bytes 262176 | tf_op jit(solution)/shard_map/all_to_all | solution.py:176
  48.1 0.7 %convert_reduce_fusion = f32[2,8,512]{2,1,0:T(8,128)} fusion(bf16[16,2,8,512]{3,2,1,0:T(8,128)(2,1)S(1)} %bitcast.32), kind=kLoop, calls=%fused_computation | loop fusion | flops 253952 | bytes 294912 | tf_op jit(solution)/shard_map/reduce_sum | solution.py:203
  (3 shorter events, 0.0 us)
Async XLA Ops:
  0.6 3.0 %copy-start.3 = (bf16[8,1024]{1,0:T(8,128)(2,1)S(1)}, bf16[8,1024]{1,0:T(8,128)(2,1)}, u32[]{:S(2)}) copy-start(bf16[8,1024]{1,0:T(8,128)(2,1)} %param.4) | copy-start | bytes 49156
  0.7 1.6 %copy-start = (bf16[128,8192]{1,0:T(8,128)(2,1)S(1)}, bf16[128,8192]{1,0:T(8,128)(2,1)}, u32[]{:S(2)}) copy-start(bf16[128,8192]{1,0:T(8,128)(2,1)} %weight_ref.1) | copy-start | bytes 6291460
  3.0 20.0 %copy-start.1 = (s32[32]{0:T(128)S(1)}, s32[32]{0:T(128)}, u32[]{:S(2)}) copy-start(s32[32]{0:T(128)} %param.6) | copy-start | bytes 388
  3.0 30.2 %copy-start.2 = (s32[32]{0:T(128)S(1)}, s32[32]{0:T(128)}, u32[]{:S(2)}) copy-start(s32[32]{0:T(128)} %param.7) | copy-start | bytes 388
  3.0 17.9 %collective-permute-start = (bf16[128,4096]{1,0:T(8,128)(2,1)S(1)}, bf16[128,4096]{1,0:T(8,128)(2,1)S(1)}, u32[]{:S(2)}, u32[]{:S(2)}) collective-permute-start(bf16[128,4096]{1,0:T(8,128)(2,1)S(1)} %get-tuple-element.12), channel_id=1, source_target_pairs={{0,1},{1,0},{2,3},{3,2},{4,5},{5,4},{6,7},{7,6},{8,9},{9,8},{10,11... | collective-permute-start | bytes 3145736 | tf_op jit(solution)/shard_map/ppermute | solution.py:124
  21.6 1.4 %collective-permute-start.1 = (f32[2,128,32]{2,1,0:T(8,128)S(1)}, f32[2,128,32]{2,1,0:T(8,128)S(1)}, u32[]{:S(2)}, u32[]{:S(2)}) collective-permute-start(f32[2,128,32]{2,1,0:T(8,128)S(1)} %half_logits.1.mine_ref), channel_id=1, source_target_pairs={{0,1},{1,0},{2,3},{3,2},{4,5},{5,4},{6,7},{7,6},{8,9},{9,8},{10,11... | collective-permute-start | bytes 98312 | tf_op jit(solution)/shard_map/ppermute | solution.py:136
  35.0 13.2 %all-to-all-start.2 = ((bf16[32,8,512]{2,1,0:T(8,128)(2,1)}), bf16[32,8,512]{2,1,0:T(8,128)(2,1)S(1)}, u32[]{:S(2)}, u32[]{:S(2)}) async-start(bf16[32,8,512]{2,1,0:T(8,128)(2,1)} %bitcast.12), calls=%async_computation.2 | async-start | bytes 524288 | tf_op jit(solution)/shard_map/all_to_all | solution.py:176
  37.6 2.1 %collective-permute-start.2 = (bf16[4,8,8,512]{3,2,1,0:T(8,128)(2,1)S(1)}, bf16[4,8,8,512]{3,2,1,0:T(8,128)(2,1)S(1)}, u32[]{:S(2)}, u32[]{:S(2)}) collective-permute-start(bf16[4,8,8,512]{3,2,1,0:T(8,128)(2,1)S(1)} %bitcast.27), channel_id=1, source_target_pairs={{0,1},{1,0},{2,3},{3,2},{4,5},{5,4},{6,7},{7,6},{8,9},{9,8},{10,11... | collective-permute-start | bytes 786440 | tf_op jit(solution)/shard_map/ppermute | solution.py:112

commit v4 on v3

v4 whole, which is shorter than its diff:
```python
import jax
import jax.numpy as jnp
from jax import lax
from jax.experimental import pallas as pl
from jax.experimental.pallas import tpu as pltpu
from jax.sharding import PartitionSpec as P


z_weight = 0.0001
BOTH = ("section", "tensor")
VMEM = pl.BlockSpec(memory_space=pltpu.VMEM)
HBM = pl.BlockSpec(memory_space=pltpu.HBM)
DMA = pltpu.SemaphoreType.DMA
SMALL = pltpu.CompilerParams(vmem_limit_bytes=16 << 20)


def this_core():
    return lax.rem(lax.axis_index("tensor"), 2)


def half_columns(block, core, half):
    return pl.ds(pl.multiple_of((2 * block + core) * half, half), half)


def first_entry(vocab_dev, other):
    index = lax.axis_index("section") * lax.axis_size("tensor") + lax.axis_index("tensor")
    if other:
        index = index + 1 - 2 * this_core()
    return index * vocab_dev


def spread_kernel(hidden_ref, out_ref):
    half = out_ref.shape[2]
    for device in range(out_ref.shape[0]):
        part = device % 2
        out_ref[device] = hidden_ref[:, part * half : (part + 1) * half]


def logits_kernel(rows_ref, weight_ref, out_ref):
    sections, tensors, rows, half = rows_ref.shape
    total = jnp.zeros(out_ref.shape, jnp.float32)
    for t in range(tensors):
        x = rows_ref[:, t].reshape(sections * rows, half)
        columns = half_columns(t, this_core(), half)
        total += lax.dot_general(
            weight_ref[:, columns], x, (((1,), (1,)), ((), ())), preferred_element_type=jnp.float32
        )
    out_ref[...] = total


def stats_kernel(mine_ref, other_ref, targets_ref, logits_ref, stats_ref):
    own = mine_ref[...] + other_ref[...]
    logits_ref[...] = own
    ids = lax.broadcasted_iota(jnp.int32, own.shape, 0) + first_entry(own.shape[0], False)
    top = jnp.max(own, axis=0, keepdims=True)
    total = jnp.sum(jnp.exp(own - top), axis=0, keepdims=True)
    picked = jnp.sum(jnp.where(ids == targets_ref[...], own, 0.0), axis=0, keepdims=True)
    parts = [top, total, picked]
    spare = stats_ref.shape[2] - 3 * top.shape[1]
    if spare:
        parts.append(jnp.zeros((1, spare), jnp.float32))
    row = jnp.concatenate(parts, axis=1)
    stats_ref[...] = jnp.broadcast_to(row[None], stats_ref.shape)


def grads_kernel(
    own_logits_ref,
    pair_logits_ref,
    log_total_ref,
    targets_ref,
    mask_ref,
    own_ref,
    pair_ref,
    dlogits_ref,
    out_ref,
    parts_ref,
    sems,
):
    sections, tensors, rows, half = out_ref.shape
    vocab_dev = own_ref.shape[0]
    core = this_core()
    log_total = log_total_ref[...]
    kept = mask_ref[...].astype(jnp.float32)
    factor = 1.0 + 2.0 * z_weight * log_total
    turned = []
    for ref, other in ((own_logits_ref, False), (pair_logits_ref, True)):
        probs = jnp.exp(ref[...] - log_total)
        ids = lax.broadcasted_iota(jnp.int32, probs.shape, 0) + first_entry(vocab_dev, other)
        hit = (ids == targets_ref[...]).astype(jnp.float32)
        dlogits = kept * (factor * probs - hit)
        if not other:
            dlogits_ref[...] = dlogits.astype(jnp.bfloat16)
        turned.append(dlogits.T.astype(jnp.bfloat16))
    copies = []
    for t in range(tensors):
        columns = half_columns(t, core, half)
        part = jnp.dot(turned[0], own_ref[:, columns], preferred_element_type=jnp.float32)
        part += jnp.dot(turned[1], pair_ref[:, columns], preferred_element_type=jnp.float32)
        parts_ref[:, t] = part.reshape(sections, rows, half).astype(jnp.bfloat16)
        copies.append(pltpu.make_async_copy(parts_ref.at[:, t], out_ref.at[:, t], sems.at[t]))
        copies[-1].start()
    for copy in copies:
        copy.wait()


def weight_kernel(
    dlogits_ref, mine_ref, other_ref, log_total_ref, picked_ref, mask_ref, out_ref, ce_ref, z_ref, blocks_ref, sems
):
    sections, tensors, rows, half = mine_ref.shape
    tokens = sections * rows
    core = this_core()
    copies = []
    for t in range(tensors):
        for ref, place in ((mine_ref, core), (other_ref, 1 - core)):
            x = ref[:, t].reshape(tokens, half)
            blocks_ref[:, half_columns(t, place, half)] = jnp.dot(
                dlogits_ref[...], x, preferred_element_type=jnp.float32
            ).astype(jnp.bfloat16)
        columns = slice(2 * t * half, 2 * (t + 1) * half)
        copies.append(pltpu.make_async_copy(blocks_ref.at[:, columns], out_ref.at[:, columns], sems.at[t]))
        copies[-1].start()
    log_total = log_total_ref[...]
    kept = mask_ref[...].astype(jnp.float32)
    ce_ref[...] = jnp.sum(kept * (log_total - picked_ref[...]), axis=1, keepdims=True) / tokens
    z_ref[...] = jnp.sum(kept * log_total * log_total, axis=1, keepdims=True) / tokens
    for copy in copies:
        copy.wait()


def body(hidden, out_weight, targets, token_mask):
    sections, tensors = lax.axis_size("section"), lax.axis_size("tensor")
    devices = sections * tensors
    vocab_dev, width = out_weight.shape
    rows, block = hidden.shape
    half = block // 2
    tokens = sections * rows
    f32, bf16 = jnp.float32, jnp.bfloat16
    swap = [(i, i ^ 1) for i in range(tensors)]
    target_row = targets.reshape(1, tokens)
    mask_row = token_mask.reshape(1, tokens)
    flops = 2 * tokens * vocab_dev * width

    pair_weight = lax.ppermute(out_weight, "tensor", swap)

    sent = pl.pallas_call(
        spread_kernel,
        out_shape=jax.ShapeDtypeStruct((devices, rows, half), bf16),
        in_specs=[VMEM],
        out_specs=VMEM,
        compiler_params=SMALL,
        name="spread_rows",
    )(hidden)
    mine = lax.all_to_all(sent, BOTH, 0, 0)
    mine = mine.reshape(sections, tensors, rows, half)
    other = lax.ppermute(mine, "tensor", swap)

    half_logits = pl.pallas_call(
        logits_kernel,
        out_shape=jax.ShapeDtypeStruct((vocab_dev, tokens), f32),
        in_specs=[VMEM, VMEM],
        out_specs=VMEM,
        compiler_params=SMALL,
        cost_estimate=pl.CostEstimate(flops=flops // 2, bytes_accessed=vocab_dev * width, transcendentals=0),
        name="half_logits",
    )
    traded = lax.ppermute(half_logits(mine, pair_weight), "tensor", swap)
    own_part = half_logits(mine, out_weight)

    lanes = -(-3 * tokens // 128) * 128
    own_logits, stats = pl.pallas_call(
        stats_kernel,
        out_shape=(
            jax.ShapeDtypeStruct((vocab_dev, tokens), f32),
            jax.ShapeDtypeStruct((devices, 1, lanes), f32),
        ),
        in_specs=[VMEM, VMEM, VMEM],
        out_specs=(VMEM, VMEM),
        compiler_params=SMALL,
        cost_estimate=pl.CostEstimate(
            flops=8 * vocab_dev * tokens, bytes_accessed=16 * vocab_dev * tokens, transcendentals=vocab_dev * tokens
        ),
        name="row_stats",
    )(own_part, traded, target_row)
    pair_logits = lax.ppermute(own_logits, "tensor", swap)

    stats = lax.all_to_all(stats, BOTH, 0, 0)
    stats = stats.reshape(devices, lanes)
    tops = stats[:, :tokens]
    totals = stats[:, tokens : 2 * tokens]
    row_top = jnp.max(tops, axis=0)
    row_total = jnp.sum(totals * jnp.exp(tops - row_top[None, :]), axis=0)
    log_total = (row_top + jnp.log(row_total)).reshape(1, tokens)
    picked = jnp.sum(stats[:, 2 * tokens : 3 * tokens], axis=0).reshape(1, tokens)

    dlogits, parts = pl.pallas_call(
        grads_kernel,
        out_shape=(
            jax.ShapeDtypeStruct((vocab_dev, tokens), bf16),
            jax.ShapeDtypeStruct((sections, tensors, rows, half), bf16),
        ),
        in_specs=[VMEM] * 7,
        out_specs=(VMEM, HBM),
        scratch_shapes=[pltpu.VMEM((sections, tensors, rows, half), bf16), DMA((tensors,))],
        compiler_params=SMALL,
        cost_estimate=pl.CostEstimate(
            flops=flops, bytes_accessed=2 * vocab_dev * width, transcendentals=2 * vocab_dev * tokens
        ),
        name="grad_parts",
    )(own_logits, pair_logits, log_total, target_row, mask_row, out_weight, pair_weight)
    shares = lax.all_to_all(parts.reshape(devices, rows, half), BOTH, 0, 0)

    scalar = jax.ShapeDtypeStruct((1, 1), f32)
    grad_weight, ce_loss, z_loss = pl.pallas_call(
        weight_kernel,
        out_shape=(jax.ShapeDtypeStruct((vocab_dev, width), bf16), scalar, scalar),
        in_specs=[VMEM] * 6,
        out_specs=(HBM, VMEM, VMEM),
        scratch_shapes=[pltpu.VMEM((vocab_dev, width), bf16), DMA((tensors,))],
        compiler_params=SMALL,
        cost_estimate=pl.CostEstimate(
            flops=flops, bytes_accessed=2 * vocab_dev * width + 2 * tokens * width, transcendentals=0
        ),
        name="grad_weight",
    )(dlogits, mine, other, log_total, picked, mask_row)

    shares = shares.reshape(devices // 2, 2, rows, half)
    grad_hidden = jnp.sum(shares.astype(f32), axis=0).transpose(1, 0, 2).reshape(rows, block)
    return (ce_loss.reshape(()), z_loss.reshape(()), grad_hidden, grad_weight)


def solution(mesh):
    placed = (P("section", "tensor"), P(("section", "tensor"), None), P(), P())
    return jax.shard_map(
        body,
        mesh=mesh,
        in_specs=placed,
        out_specs=(P(), P(), P("section", "tensor"), P(("section", "tensor"), None)),
        check_vma=False,
    )
```

time: 51.3 us -> 48.6 us (0.947)
  waiting for transfers between devices: 5.37 us -> 15.7 us
  blocking collectives: 26.7 us -> 17.3 us
  between operations: 4.3 us -> 0.75 us
  Pallas kernels: 8.19 us -> 4.86 us
  starting transfers between devices: 3.4 us -> 6.13 us
  local copies, waits for them, and re-layouts: 1.63 us -> 2.75 us
  other arithmetic: 1.46 us -> 0.78 us
    all_to_all x1 -> x0, blocking collectives: 9.38 us -> none  [body(): stats = lax.all_to_all(stats, BOTH, 0, 0).reshape(devices, lanes)]
    all_to_all x0 -> x1, waiting for transfers between devices: none -> 6.92 us  [body(): stats = lax.all_to_all(stats, BOTH, 0, 0)]
    all_to_all x1, waiting for transfers between devices: 4.03 us -> 6.87 us  [body(): shares = lax.all_to_all(parts.reshape(devices, rows, half), BOTH, 0, 0)]
    pallas_call x4 -> x5, Pallas kernels: 6.48 us -> 3.68 us  [the longest x1 2.09 us: body(): pl.pallas_call(weight_kernel, out_shape=(jax.ShapeDtypeStruct((vocab_dev,...]
    all_to_all x0 -> x1, starting transfers between devices: none -> 2.54 us  [body(): stats = lax.all_to_all(stats, BOTH, 0, 0)]
    ppermute x1, waiting for transfers between devices: 0.01 us -> 1.42 us  [body(): other = lax.ppermute(mine, 'tensor', swap)]
    unnamed x8 -> x12, local copies, waits for them, and re-layouts: 1.61 us -> 2.75 us
    ppermute x2 -> x3, waiting for transfers between devices: 1.34 us -> 0.44 us  [the longest x1 0.43 us: body(): traded = lax.ppermute(half_logits(mine, pair_weight), 'tensor', swap)]
  transfers between devices with their start and end apart: 4 -> 6, of which waited for: 2 -> 4; matrix products, arithmetic and copies ran while one was open for 1% -> 0% of each run, Pallas kernels for 9% -> 5%
where the time goes in v4:
time: 48.6 us; the launch traced here: 48.2 us
  blocking collectives  17.3 us (36%)
  waiting for transfers between devices  15.7 us (32%)
  starting transfers between devices  6.13 us (13%)
  Pallas kernels  4.86 us (10%)
  local copies, waits for them, and re-layouts  2.75 us (6%)
  other arithmetic  0.78 us (2%)
  between operations  0.75 us (2%)
    all_to_all x1, blocking collectives, body(): mine = lax.all_to_all(sent, BOTH, 0, 0)  17.3 us
    all_to_all x1, waiting for transfers between devices, body(): stats = lax.all_to_all(stats, BOTH, 0, 0)  6.92 us
    all_to_all x1, waiting for transfers between devices, body(): shares = lax.all_to_all(parts.reshape(devices, rows, half), BOTH, 0, 0)  6.87 us
    unnamed x12, local copies, waits for them, and re-layouts  2.75 us
    all_to_all x1, starting transfers between devices, body(): shares = lax.all_to_all(parts.reshape(devices, rows, half), BOTH, 0, 0)  2.6 us
    all_to_all x1, starting transfers between devices, body(): stats = lax.all_to_all(stats, BOTH, 0, 0)  2.54 us
    pallas_call x1, Pallas kernels, body(): pl.pallas_call(weight_kernel, out_shape=(jax.ShapeDtypeStruct((vocab_dev,...  2.09 us
    ppermute x1, waiting for transfers between devices, body(): other = lax.ppermute(mine, 'tensor', swap)  1.42 us
  transfers between devices with their start and end apart: 6, of which 4 were waited for; matrix products, arithmetic and copies ran while one was open for 0% of the time, Pallas kernels for 5%

profile of v4, /device:TPU:0, one launch (start us, length us, event | category | flops | bytes accessed | tf_op | source)
XLA Modules:
  0.0 48.2 jit_solution(16102664607748449923)
XLA Ops:
  0.6 0.0 copy-start
  0.6 0.6 %collective-permute-start = (bf16[128,8192]{1,0:T(8,128)(2,1)}, bf16[128,8192]{1,0:T(8,128)(2,1)S(1)}, u32[]{:S(2)}, u32[]{:S(2)}) collective-permute-start(bf16[128,8192]{1,0:T(8,128)(2,1)} %own_ref.1), channel_id=1, source_target_pairs={{0,1},{1,0},{2,3},{3,2},{4,5},{5,4},{6,7},{7,6},{8,9},{9,8},{10,11... | collective-permute-start | bytes 6291464 | tf_op jit(solution)/shard_map/ppermute | solution.py:143
  1.2 0.0 copy-start.3
  1.2 0.8 %copy-done.3 = bf16[8,1024]{1,0:T(8,128)(2,1)S(1)} copy-done((bf16[8,1024]{1,0:T(8,128)(2,1)S(1)}, bf16[8,1024]{1,0:T(8,128)(2,1)}, u32[]{:S(2)}) %copy-start.3) | copy-done | bytes 16408
  2.0 17.3 %all_to_all.15 = bf16[32,8,512]{2,1,0:T(8,128)(2,1)S(1)} all-to-all(bf16[32,8,512]{2,1,0:T(8,128)(2,1)S(1)} %spread_rows.1), channel_id=1, replica_groups=mesh['section'=4,'tensor'=8] {'section','tensor'}, dimensions={0} | all-to-all | bytes 524288 | tf_op jit(solution)/shard_map/all_to_all | solution.py:153
  19.3 0.0 collective-permute-done.weight_ref.pair_ref
  19.3 0.0 copy-start.1
  19.3 0.0 copy-start.4
  19.3 0.0 copy-start.5
  19.3 0.4 half_logits.3
  19.7 0.1 collective-permute-start.1
  19.8 0.0 copy-done
  19.8 0.4 half_logits.2.mine_ref
  20.3 0.4 copy-done.1
  20.6 0.4 collective-permute-done.1.other_ref
  21.1 0.0 copy-done.4
  21.1 0.7 %row_stats.1 = (f32[128,32]{1,0:T(8,128)S(1)}, f32[32,1,128]{2,1,0:T(1,128)}) custom-call(f32[128,32]{1,0:T(8,128)S(1)} %half_logits.2.mine_ref, f32[128,32]{1,0:T(8,128)S(1)} %collective-permute-done.1.other_ref, s32[1,32]{1,0:T(1,128)S(1)} %bitcast.19), custom_call_target="tpu_custom_call" | custom-call | flops 32768 | bytes 65536 | tf_op jit(solution)/shard_map/row_stats/pallas_call | solution.py:170
  21.8 2.5 %all-to-all-start.1 = ((f32[32,1,128]{2,1,0:T(1,128)}), f32[32,1,128]{2,1,0:T(1,128)S(1)}, u32[]{:S(2)}, u32[]{:S(2)}) async-start(f32[32,1,128]{2,1,0:T(1,128)} %get-tuple-element.12), calls=%async_computation.1 | async-start | bytes 32768 | tf_op jit(solution)/shard_map/all_to_all | solution.py:186
  24.3 0.2 collective-permute-start.2
  24.5 6.9 %all-to-all-done.1 = f32[32,1,128]{2,1,0:T(1,128)S(1)} async-done(((f32[32,1,128]{2,1,0:T(1,128)}), f32[32,1,128]{2,1,0:T(1,128)S(1)}, u32[]{:S(2)}, u32[]{:S(2)}) %all-to-all-start.1) | async-done | bytes 16416 | tf_op jit(solution)/shard_map/all_to_all | solution.py:186
  31.5 0.1 slice_reduce_fusion
  31.6 0.0 collective-permute-done.2.pair_logits_ref
  31.6 0.0 copy-done.5
  31.6 0.0 copy-start.2
  31.6 1.6 %copy-done.2 = bf16[128,8192]{1,0:T(8,128)(2,1)S(1)} copy-done((bf16[128,8192]{1,0:T(8,128)(2,1)S(1)}, bf16[128,8192]{1,0:T(8,128)(2,1)}, u32[]{:S(2)}) %copy-start.2) | copy-done | bytes 2097176
  33.2 1.2 %grad_parts.1 = (bf16[128,32]{1,0:T(8,128)(2,1)S(1)}, bf16[4,8,8,512]{3,2,1,0:T(8,128)(2,1)}) custom-call(f32[128,32]{1,0:T(8,128)S(1)} %get-tuple-element.11.own_logits_ref, f32[128,32]{1,0:T(8,128)S(1)} %collective-permute-done.2.pair_logits_ref, f32[1,32]{1,0:T(1,128)S(1)} %add_bitcast_fusion.log_total_ref, s32[1,32]{1,0:T(1,128)S(1)} %bitcast.20, ...), custom_call_target="tpu_custom_call" | custom-call | flops 67108864 | bytes 2097152 | tf_op jit(solution)/shard_map/grad_parts/pallas_call | solution.py:195
  34.4 2.6 %all-to-all-start.2 = ((bf16[32,8,512]{2,1,0:T(8,128)(2,1)}), bf16[32,8,512]{2,1,0:T(8,128)(2,1)S(1)}, u32[]{:S(2)}, u32[]{:S(2)}) async-start(bf16[32,8,512]{2,1,0:T(8,128)(2,1)} %bitcast.8), calls=%async_computation.2 | async-start | bytes 524288 | tf_op jit(solution)/shard_map/all_to_all | solution.py:210
  37.0 0.2 collective-permute-start.3
  37.2 1.4 %collective-permute-done.3.other_ref = bf16[4,8,8,512]{3,2,1,0:T(8,128)(2,1)S(1)} collective-permute-done((bf16[4,8,8,512]{3,2,1,0:T(8,128)(2,1)S(1)}, bf16[4,8,8,512]{3,2,1,0:T(8,128)(2,1)S(1)}, u32[]{:S(2)}, u32[]{:S(2)}) %collective-permute-start.3) | collective-permute-done | bytes 262176 | tf_op jit(solution)/shard_map/ppermute | solution.py:155
  38.6 2.1 %grad_weight.1 = (bf16[128,8192]{1,0:T(8,128)(2,1)}, f32[1,1]{1,0:T(1,128)}, f32[1,1]{1,0:T(1,128)}) custom-call(bf16[128,32]{1,0:T(8,128)(2,1)S(1)} %get-tuple-element.13.dlogits_ref, bf16[4,8,8,512]{3,2,1,0:T(8,128)(2,1)S(1)} %bitcast.18, bf16[4,8,8,512]{3,2,1,0:T(8,128)(2,1)S(1)} %collective-permute-done.3.other_ref, ...), custom_call_target="tpu_custom_call" | custom-call | flops 67108864 | bytes 2621440 | tf_op jit(solution)/shard_map/grad_weight/pallas_call | solution.py:213
  40.7 6.9 %all-to-all-done.2 = bf16[32,8,512]{2,1,0:T(8,128)(2,1)S(1)} async-done(((bf16[32,8,512]{2,1,0:T(8,128)(2,1)}), bf16[32,8,512]{2,1,0:T(8,128)(2,1)S(1)}, u32[]{:S(2)}, u32[]{:S(2)}) %all-to-all-start.2) | async-done | bytes 262176 | tf_op jit(solution)/shard_map/all_to_all | solution.py:210
  47.6 0.7 %convert_reduce_fusion = f32[2,8,512]{2,1,0:T(8,128)} fusion(bf16[16,2,8,512]{3,2,1,0:T(8,128)(2,1)S(1)} %bitcast.24), kind=kLoop, calls=%fused_computation | loop fusion | flops 253952 | bytes 294912 | tf_op jit(solution)/shard_map/reduce_sum | solution.py:227
  (3 shorter events, 0.0 us)
Async XLA Ops:
  0.6 19.2 %copy-start = (bf16[128,8192]{1,0:T(8,128)(2,1)S(1)}, bf16[128,8192]{1,0:T(8,128)(2,1)}, u32[]{:S(2)}) copy-start(bf16[128,8192]{1,0:T(8,128)(2,1)} %own_ref.1) | copy-start | bytes 6291460
  0.6 18.7 %collective-permute-start = (bf16[128,8192]{1,0:T(8,128)(2,1)}, bf16[128,8192]{1,0:T(8,128)(2,1)S(1)}, u32[]{:S(2)}, u32[]{:S(2)}) collective-permute-start(bf16[128,8192]{1,0:T(8,128)(2,1)} %own_ref.1), channel_id=1, source_target_pairs={{0,1},{1,0},{2,3},{3,2},{4,5},{5,4},{6,7},{7,6},{8,9},{9,8},{10,11... | collective-permute-start | bytes 6291464 | tf_op jit(solution)/shard_map/ppermute | solution.py:143
  1.2 0.8 %copy-start.3 = (bf16[8,1024]{1,0:T(8,128)(2,1)S(1)}, bf16[8,1024]{1,0:T(8,128)(2,1)}, u32[]{:S(2)}) copy-start(bf16[8,1024]{1,0:T(8,128)(2,1)} %hidden_ref.1) | copy-start | bytes 49156
  19.3 1.3 %copy-start.1 = (bf16[128,8192]{1,0:T(8,128)(2,1)}, bf16[128,8192]{1,0:T(8,128)(2,1)S(1)}, u32[]{:S(2)}) copy-start(bf16[128,8192]{1,0:T(8,128)(2,1)S(1)} %collective-permute-done.weight_ref.pair_ref) | copy-start | bytes 6291460
  19.3 1.8 %copy-start.4 = (s32[32]{0:T(128)S(1)}, s32[32]{0:T(128)}, u32[]{:S(2)}) copy-start(s32[32]{0:T(128)} %param.6) | copy-start | bytes 388
  19.3 12.3 %copy-start.5 = (s32[32]{0:T(128)S(1)}, s32[32]{0:T(128)}, u32[]{:S(2)}) copy-start(s32[32]{0:T(128)} %param.7) | copy-start | bytes 388
  19.7 1.3 %collective-permute-start.1 = (f32[128,32]{1,0:T(8,128)S(1)}, f32[128,32]{1,0:T(8,128)S(1)}, u32[]{:S(2)}, u32[]{:S(2)}) collective-permute-start(f32[128,32]{1,0:T(8,128)S(1)} %half_logits.3), channel_id=1, source_target_pairs={{0,1},{1,0},{2,3},{3,2},{4,5},{5,4},{6,7},{7,6},{8,9},{9,8},{10,11... | collective-permute-start | bytes 49160 | tf_op jit(solution)/shard_map/ppermute | solution.py:166
  21.8 9.7 %all-to-all-start.1 = ((f32[32,1,128]{2,1,0:T(1,128)}), f32[32,1,128]{2,1,0:T(1,128)S(1)}, u32[]{:S(2)}, u32[]{:S(2)}) async-start(f32[32,1,128]{2,1,0:T(1,128)} %get-tuple-element.12), calls=%async_computation.1 | async-start | bytes 32768 | tf_op jit(solution)/shard_map/all_to_all | solution.py:186
  24.3 7.2 %collective-permute-start.2 = (f32[128,32]{1,0:T(8,128)S(1)}, f32[128,32]{1,0:T(8,128)S(1)}, u32[]{:S(2)}, u32[]{:S(2)}) collective-permute-start(f32[128,32]{1,0:T(8,128)S(1)} %get-tuple-element.11.own_logits_ref), channel_id=1, source_target_pairs={{0,1},{1,0},{2,3},{3,2},{4,5},{5,4},{6,7},{7,6},{8,9},{9,8},{10,11... | collective-permute-start | bytes 49160 | tf_op jit(solution)/shard_map/ppermute | solution.py:184
  31.6 1.6 %copy-start.2 = (bf16[128,8192]{1,0:T(8,128)(2,1)S(1)}, bf16[128,8192]{1,0:T(8,128)(2,1)}, u32[]{:S(2)}) copy-start(bf16[128,8192]{1,0:T(8,128)(2,1)} %copy-done.1) | copy-start | bytes 6291460
  34.4 13.2 %all-to-all-start.2 = ((bf16[32,8,512]{2,1,0:T(8,128)(2,1)}), bf16[32,8,512]{2,1,0:T(8,128)(2,1)S(1)}, u32[]{:S(2)}, u32[]{:S(2)}) async-start(bf16[32,8,512]{2,1,0:T(8,128)(2,1)} %bitcast.8), calls=%async_computation.2 | async-start | bytes 524288 | tf_op jit(solution)/shard_map/all_to_all | solution.py:210
  37.0 1.6 %collective-permute-start.3 = (bf16[4,8,8,512]{3,2,1,0:T(8,128)(2,1)S(1)}, bf16[4,8,8,512]{3,2,1,0:T(8,128)(2,1)S(1)}, u32[]{:S(2)}, u32[]{:S(2)}) collective-permute-start(bf16[4,8,8,512]{3,2,1,0:T(8,128)(2,1)S(1)} %bitcast.17), channel_id=1, source_target_pairs={{0,1},{1,0},{2,3},{3,2},{4,5},{5,4},{6,7},{7,6},{8,9},{9,8},{10,11... | collective-permute-start | bytes 786440 | tf_op jit(solution)/shard_map/ppermute | solution.py:155

commit v5 on v4

v5 whole, which is shorter than its diff:
```python
import jax
import jax.numpy as jnp
from jax import lax
from jax.experimental import pallas as pl
from jax.experimental.pallas import tpu as pltpu
from jax.sharding import PartitionSpec as P


z_weight = 0.0001
BOTH = ("section", "tensor")
LANES = 128
VMEM = pl.BlockSpec(memory_space=pltpu.VMEM)
HBM = pl.BlockSpec(memory_space=pltpu.HBM)
DMA = pltpu.SemaphoreType.DMA
SMALL = pltpu.CompilerParams(vmem_limit_bytes=16 << 20)
F32, BF16 = jnp.float32, jnp.bfloat16


def tiles_of(count):
    return -(-count // LANES)


def this_core():
    return lax.rem(lax.axis_index("tensor"), 2)


def half_columns(block, core, half):
    return pl.ds(pl.multiple_of((2 * block + core) * half, half), half)


def target_hits(shape, targets, other):
    index = lax.axis_index("section") * lax.axis_size("tensor") + lax.axis_index("tensor")
    if other:
        index = index + 1 - 2 * this_core()
    return lax.broadcasted_iota(jnp.int32, shape, 0) + index * shape[0] == targets


def spread_kernel(hidden_ref, out_ref):
    half = out_ref.shape[2]
    for device in range(out_ref.shape[0]):
        part = device % 2
        out_ref[device] = hidden_ref[:, part * half : (part + 1) * half]


def logits_kernel(rows_ref, weight_ref, out_ref):
    sections, tensors, rows, half = rows_ref.shape
    core = this_core()
    total = jnp.zeros(out_ref.shape, F32)
    for t in range(tensors):
        x = rows_ref[:, t].reshape(sections * rows, half)
        total += lax.dot_general(
            weight_ref[:, half_columns(t, core, half)], x, (((1,), (1,)), ((), ())), preferred_element_type=F32
        )
    out_ref[...] = total


def parts_kernel(
    own_mine_ref, own_other_ref, pair_mine_ref, pair_other_ref, targets_ref, own_ref, pair_ref, logits_ref, out_ref
):
    vocab_dev, tokens = own_mine_ref.shape
    sections, tensors, _, rows, _ = out_ref.shape
    half = own_ref.shape[1] // tensors // 2
    pieces = half // LANES
    core = this_core()
    targets = targets_ref[...]
    logits = (own_mine_ref[...] + own_other_ref[...], pair_mine_ref[...] + pair_other_ref[...])
    logits_ref[...] = logits[0]
    hits = [target_hits((vocab_dev, tokens), targets, other) for other in (False, True)]
    rest = [jnp.where(hit, -jnp.inf, x) for hit, x in zip(hits, logits)]
    top = jnp.maximum(*[jnp.max(x, axis=0, keepdims=True) for x in rest])
    shares = [jnp.exp(x - top) for x in rest]
    total = sum(jnp.sum(x, axis=0, keepdims=True) for x in shares)
    picked = sum(jnp.sum(jnp.where(hit, x, 0.0), axis=0, keepdims=True) for hit, x in zip(hits, logits))

    turned = []
    for share, hit in zip(shares, hits):
        share = share.T
        coarse = share.astype(BF16)
        fine = (share - coarse.astype(F32)).astype(BF16)
        turned.append(jnp.concatenate([coarse, fine, hit.astype(F32).T.astype(BF16)], axis=0))
    for t in range(tensors):
        columns = half_columns(t, core, half)
        part = jnp.dot(turned[0], own_ref[:, columns], preferred_element_type=F32)
        part += jnp.dot(turned[1], pair_ref[:, columns], preferred_element_type=F32)
        weighted = (part[:tokens] + part[tokens : 2 * tokens]).reshape(sections, rows, half).astype(BF16)
        targeted = part[2 * tokens :].reshape(sections, rows, half).astype(BF16)
        for j in range(pieces):
            lanes = slice(j * LANES, (j + 1) * LANES)
            out_ref[:, t, j] = weighted[:, :, lanes]
            out_ref[:, t, pieces + j] = targeted[:, :, lanes]

    spare = tiles_of(3 * tokens) * LANES - 3 * tokens
    row = [top, total, picked] + ([jnp.zeros((1, spare), F32)] if spare else [])
    row = jnp.concatenate(row, axis=1)
    digits = []
    for _ in range(3):
        digits.append(row.astype(BF16).astype(F32))
        row = row - digits[-1]
    digits.append(jnp.zeros((rows - 3, row.shape[1]), F32))
    digits = jnp.concatenate(digits, axis=0).astype(BF16)
    for j in range(tiles_of(3 * tokens)):
        tile = digits[:, j * LANES : (j + 1) * LANES]
        for t in range(tensors):
            out_ref[:, t, 2 * pieces + j] = jnp.broadcast_to(tile[None], (sections, rows, LANES))


def totals_kernel(
    parts_ref, logits_ref, targets_ref, mask_ref, dlogits_ref, scales_ref, log_total_ref, picked_ref, table_ref
):
    chips = table_ref.shape[0]
    tokens = log_total_ref.shape[1]
    first = parts_ref.shape[1] - tiles_of(3 * tokens)
    for k in range(chips):
        for j in range(tiles_of(3 * tokens)):
            tile = parts_ref[2 * k, first + j].astype(F32)
            table_ref[k : k + 1, j * LANES : (j + 1) * LANES] = jnp.sum(tile, axis=0, keepdims=True)
    table = table_ref[...]
    tops = table[:, :tokens]
    totals = table[:, tokens : 2 * tokens]
    picked = jnp.sum(table[:, 2 * tokens : 3 * tokens], axis=0, keepdims=True)
    row_top = jnp.maximum(jnp.max(tops, axis=0, keepdims=True), picked)
    row_total = jnp.sum(totals * jnp.exp(tops - row_top), axis=0, keepdims=True) + jnp.exp(picked - row_top)
    log_total = row_top + jnp.log(row_total)
    kept = mask_ref[...].astype(F32)
    factor = 1.0 + 2.0 * z_weight * log_total
    hit = target_hits(logits_ref.shape, targets_ref[...], False).astype(F32)
    dlogits_ref[...] = (kept * (factor * jnp.exp(logits_ref[...] - log_total) - hit)).astype(BF16)
    log_total_ref[...] = log_total
    picked_ref[...] = picked

    scales = (kept * (factor * jnp.exp(tops - log_total))).astype(BF16).astype(F32)
    scale = (kept * (factor * jnp.exp(picked - log_total) - 1.0)).astype(BF16).astype(F32)
    spare = scales_ref.shape[1] - chips - 1
    scales_ref[...] = jnp.concatenate([scales, scale, jnp.zeros((spare, tokens), F32)], axis=0).T


def finish_kernel(
    dlogits_ref,
    mine_ref,
    other_ref,
    parts_ref,
    scales_ref,
    log_total_ref,
    picked_ref,
    mask_ref,
    weight_grad_ref,
    hidden_grad_ref,
    ce_ref,
    z_ref,
    blocks_ref,
    sems,
):
    sections, tensors, rows, half = mine_ref.shape
    tokens = sections * rows
    chips = sections * tensors // 2
    pieces = half // LANES
    core = this_core()
    dlogits = dlogits_ref[...]
    copies = []
    for t in range(tensors):
        for ref, place in ((mine_ref, core), (other_ref, 1 - core)):
            x = ref[:, t].reshape(tokens, half)
            blocks_ref[:, half_columns(t, place, half)] = jnp.dot(
                dlogits, x, preferred_element_type=F32
            ).astype(BF16)
        columns = slice(2 * t * half, 2 * (t + 1) * half)
        copies.append(pltpu.make_async_copy(blocks_ref.at[:, columns], weight_grad_ref.at[:, columns], sems.at[t]))
        copies[-1].start()

    here = scales_ref[pl.ds(pl.multiple_of(lax.axis_index("section") * rows, rows), rows), :]
    for part in range(2):
        for j in range(pieces):
            weighted = jnp.zeros((rows, LANES), F32)
            targeted = jnp.zeros((rows, LANES), F32)
            for k in range(chips):
                weighted += here[:, k : k + 1] * parts_ref[2 * k + part, j].astype(F32)
                targeted += parts_ref[2 * k + part, pieces + j].astype(F32)
            start = part * half + j * LANES
            hidden_grad_ref[:, start : start + LANES] = weighted + here[:, chips : chips + 1] * targeted

    log_total = log_total_ref[...]
    kept = mask_ref[...].astype(F32)
    ce_ref[...] = jnp.sum(kept * (log_total - picked_ref[...]), axis=1, keepdims=True) / tokens
    z_ref[...] = jnp.sum(kept * log_total * log_total, axis=1, keepdims=True) / tokens
    for copy in copies:
        copy.wait()


def body(hidden, out_weight, targets, token_mask):
    sections, tensors = lax.axis_size("section"), lax.axis_size("tensor")
    devices = sections * tensors
    vocab_dev, width = out_weight.shape
    rows, block = hidden.shape
    half = block // 2
    tokens = sections * rows
    swap = [(i, i ^ 1) for i in range(tensors)]
    target_row = targets.reshape(1, tokens)
    mask_row = token_mask.reshape(1, tokens)
    flops = 2 * tokens * vocab_dev * width
    tiles = 2 * (half // LANES) + tiles_of(3 * tokens)

    pair_weight = lax.ppermute(out_weight, "tensor", swap)
    sent = pl.pallas_call(
        spread_kernel,
        out_shape=jax.ShapeDtypeStruct((devices, rows, half), BF16),
        in_specs=[VMEM],
        out_specs=VMEM,
        compiler_params=SMALL,
        name="spread_rows",
    )(hidden)
    mine = lax.all_to_all(sent, BOTH, 0, 0)
    mine = mine.reshape(sections, tensors, rows, half)

    half_logits = pl.pallas_call(
        logits_kernel,
        out_shape=jax.ShapeDtypeStruct((vocab_dev, tokens), F32),
        in_specs=[VMEM] * 2,
        out_specs=VMEM,
        compiler_params=SMALL,
        cost_estimate=pl.CostEstimate(flops=flops // 2, bytes_accessed=vocab_dev * width, transcendentals=0),
        name="half_logits",
    )
    pair_mine = half_logits(mine, pair_weight)
    own_other = lax.ppermute(pair_mine, "tensor", swap)
    own_mine = half_logits(mine, out_weight)
    pair_other = lax.ppermute(own_mine, "tensor", swap)
    other = lax.ppermute(mine, "tensor", swap)

    logits, parts = pl.pallas_call(
        parts_kernel,
        out_shape=(
            jax.ShapeDtypeStruct((vocab_dev, tokens), F32),
            jax.ShapeDtypeStruct((sections, tensors, tiles, rows, LANES), BF16),
        ),
        in_specs=[VMEM] * 7,
        out_specs=(VMEM, VMEM),
        compiler_params=SMALL,
        cost_estimate=pl.CostEstimate(
            flops=3 * flops, bytes_accessed=2 * vocab_dev * width, transcendentals=2 * vocab_dev * tokens
        ),
        name="grad_parts",
    )(own_mine, own_other, pair_mine, pair_other, target_row, out_weight, pair_weight)
    parts = lax.all_to_all(parts.reshape(devices, tiles, rows, LANES), BOTH, 0, 0)

    chips = devices // 2
    row = jax.ShapeDtypeStruct((1, tokens), F32)
    dlogits, scales, log_total, picked = pl.pallas_call(
        totals_kernel,
        out_shape=(
            jax.ShapeDtypeStruct((vocab_dev, tokens), BF16),
            jax.ShapeDtypeStruct((tokens, tiles_of(chips + 1) * LANES), F32),
            row,
            row,
        ),
        in_specs=[VMEM] * 4,
        out_specs=(VMEM,) * 4,
        scratch_shapes=[pltpu.VMEM((chips, tiles_of(3 * tokens) * LANES), F32)],
        compiler_params=SMALL,
        cost_estimate=pl.CostEstimate(
            flops=8 * vocab_dev * tokens, bytes_accessed=16 * vocab_dev * tokens, transcendentals=vocab_dev * tokens
        ),
        name="totals",
    )(parts, logits, target_row, mask_row)

    scalar = jax.ShapeDtypeStruct((1, 1), F32)
    grad_weight, grad_hidden, ce_loss, z_loss = pl.pallas_call(
        finish_kernel,
        out_shape=(
            jax.ShapeDtypeStruct((vocab_dev, width), BF16),
            jax.ShapeDtypeStruct((rows, block), F32),
            scalar,
            scalar,
        ),
        in_specs=[VMEM] * 8,
        out_specs=(HBM, VMEM, VMEM, VMEM),
        scratch_shapes=[pltpu.VMEM((vocab_dev, width), BF16), DMA((tensors,))],
        compiler_params=SMALL,
        cost_estimate=pl.CostEstimate(
            flops=flops, bytes_accessed=2 * vocab_dev * width + 2 * tokens * width, transcendentals=0
        ),
        name="finish",
    )(dlogits, mine, other, parts, scales, log_total, picked, mask_row)
    return (ce_loss.reshape(()), z_loss.reshape(()), grad_hidden, grad_weight)


def solution(mesh):
    placed = (P("section", "tensor"), P(("section", "tensor"), None), P(), P())
    return jax.shard_map(
        body,
        mesh=mesh,
        in_specs=placed,
        out_specs=(P(), P(), P("section", "tensor"), P(("section", "tensor"), None)),
        check_vma=False,
    )
```

time: 48.6 us -> 47.2 us (0.971)
  starting transfers between devices: 6.13 us -> 3.97 us
  waiting for transfers between devices: 15.7 us -> 17.5 us
  other arithmetic: 0.78 us -> 0 us
    all_to_all x2 -> x1, waiting for transfers between devices: 13.8 us -> 16.6 us  [body(): lax.all_to_all(parts.reshape(devices, tiles, rows, LANES), BOTH, 0, 0)]
    all_to_all x2 -> x1, starting transfers between devices: 5.14 us -> 2.61 us  [body(): lax.all_to_all(parts.reshape(devices, tiles, rows, LANES), BOTH, 0, 0)]
    ppermute x1, waiting for transfers between devices: 1.42 us -> 0.01 us  [body(): other = lax.ppermute(mine, 'tensor', swap)]
    reduce_sum x2 -> x0, other arithmetic: 0.75 us -> none  [the longest x1 0.66 us: body(): jnp.sum(shares.astype(f32), axis=0).transpose(1, 0, 2).reshape(rows, block)]
    unnamed x12 -> x10, local copies, waits for them, and re-layouts: 2.75 us -> 2.32 us
  transfers between devices with their start and end apart: 6 -> 5, of which waited for: 4 -> 3; matrix products, arithmetic and copies ran while one was open for 0% -> 0% of each run, Pallas kernels for 5% -> 3%
where the time goes in v5:
time: 47.2 us; the launch traced here: 46.9 us
  waiting for transfers between devices  17.5 us (37%)
  blocking collectives  17.3 us (37%)
  Pallas kernels  5.09 us (11%)
  starting transfers between devices  3.97 us (8%)
  local copies, waits for them, and re-layouts  2.32 us (5%)
  between operations  0.68 us (1%)
    all_to_all x1, blocking collectives, body(): mine = lax.all_to_all(sent, BOTH, 0, 0)  17.3 us
    all_to_all x1, waiting for transfers between devices, body(): lax.all_to_all(parts.reshape(devices, tiles, rows, LANES), BOTH, 0, 0)  16.6 us
    all_to_all x1, starting transfers between devices, body(): lax.all_to_all(parts.reshape(devices, tiles, rows, LANES), BOTH, 0, 0)  2.61 us
    unnamed x10, local copies, waits for them, and re-layouts  2.32 us
    pallas_call x1, Pallas kernels, body(): pl.pallas_call(finish_kernel, out_shape=(jax.ShapeDtypeStruct((vocab_dev,...  2.21 us
    pallas_call x1, Pallas kernels, body(): pl.pallas_call(parts_kernel, out_shape=(jax.ShapeDtypeStruct((vocab_dev,...  1.5 us
  transfers between devices with their start and end apart: 5, of which 3 were waited for; matrix products, arithmetic and copies ran while one was open for 0% of the time, Pallas kernels for 3%

profile of v5, /device:TPU:0, one launch (start us, length us, event | category | flops | bytes accessed | tf_op | source)
XLA Modules:
  0.0 46.9 jit_solution(9927223502611677554)
XLA Ops:
  0.6 0.6 %collective-permute-start = (bf16[128,8192]{1,0:T(8,128)(2,1)}, bf16[128,8192]{1,0:T(8,128)(2,1)S(1)}, u32[]{:S(2)}, u32[]{:S(2)}) collective-permute-start(bf16[128,8192]{1,0:T(8,128)(2,1)} %own_ref.1), channel_id=1, source_target_pairs={{0,1},{1,0},{2,3},{3,2},{4,5},{5,4},{6,7},{7,6},{8,9},{9,8},{10,11... | collective-permute-start | bytes 6291464 | tf_op jit(solution)/shard_map/ppermute | solution.py:202
  1.2 0.0 copy-start.2
  1.2 0.7 %copy-done.2 = bf16[8,1024]{1,0:T(8,128)(2,1)S(1)} copy-done((bf16[8,1024]{1,0:T(8,128)(2,1)S(1)}, bf16[8,1024]{1,0:T(8,128)(2,1)}, u32[]{:S(2)}) %copy-start.2) | copy-done | bytes 16408
  1.9 17.3 %all_to_all.10 = bf16[32,8,512]{2,1,0:T(8,128)(2,1)S(1)} all-to-all(bf16[32,8,512]{2,1,0:T(8,128)(2,1)S(1)} %spread_rows.1), channel_id=1, replica_groups=mesh['section'=4,'tensor'=8] {'section','tensor'}, dimensions={0} | all-to-all | bytes 524288 | tf_op jit(solution)/shard_map/all_to_all | solution.py:211
  19.3 0.0 copy-start
  19.3 1.6 %copy-done = bf16[128,8192]{1,0:T(8,128)(2,1)S(1)} copy-done((bf16[128,8192]{1,0:T(8,128)(2,1)S(1)}, bf16[128,8192]{1,0:T(8,128)(2,1)}, u32[]{:S(2)}) %copy-start) | copy-done | bytes 2097176
  20.8 0.0 copy-start.1
  20.8 0.0 copy-start.4
  20.9 0.4 half_logits.2.own_mine_ref
  21.3 0.1 collective-permute-start.2
  21.3 0.0 collective-permute-done.weight_ref.pair_ref
  21.4 0.4 half_logits.3.pair_mine_ref
  21.8 0.6 %collective-permute-start.1 = (f32[128,32]{1,0:T(8,128)S(1)}, f32[128,32]{1,0:T(8,128)S(1)}, u32[]{:S(2)}, u32[]{:S(2)}) collective-permute-start(f32[128,32]{1,0:T(8,128)S(1)} %half_logits.3.pair_mine_ref), channel_id=1, source_target_pairs={{0,1},{1,0},{2,3},{3,2},{4,5},{5,4},{6,7},{7,6},{8,9},{9,8},{10,11... | collective-permute-start | bytes 49160 | tf_op jit(solution)/shard_map/ppermute | solution.py:224
  22.3 0.2 collective-permute-done.2.pair_other_ref
  22.6 0.7 %collective-permute-done.1.own_other_ref = f32[128,32]{1,0:T(8,128)S(1)} collective-permute-done((f32[128,32]{1,0:T(8,128)S(1)}, f32[128,32]{1,0:T(8,128)S(1)}, u32[]{:S(2)}, u32[]{:S(2)}) %collective-permute-start.1) | collective-permute-done | bytes 16416 | tf_op jit(solution)/shard_map/ppermute | solution.py:224
  23.2 0.0 copy-done.1
  23.2 0.0 copy-done.4
  23.2 0.0 copy-start.3
  23.2 1.5 %grad_parts.1 = (f32[128,32]{1,0:T(8,128)S(1)}, bf16[4,8,9,8,128]{4,3,2,1,0:T(8,128)(2,1)}) custom-call(f32[128,32]{1,0:T(8,128)S(1)} %half_logits.2.own_mine_ref, f32[128,32]{1,0:T(8,128)S(1)} %collective-permute-done.1.own_other_ref, f32[128,32]{1,0:T(8,128)S(1)} %half_logits.3.pair_mine_ref, f32[128,32]{1,0:T(8,128)S(1)} %collective-permute-done.2.pair_other_ref, ...), custom_call_target="tpu_custom_call" | custom-call | flops 201326592 | bytes 2097152 | tf_op jit(solution)/shard_map/grad_parts/pallas_call | solution.py:229
  24.8 2.6 %all-to-all-start.1 = ((bf16[32,9,8,128]{3,2,1,0:T(8,128)(2,1)}), bf16[32,9,8,128]{3,2,1,0:T(8,128)(2,1)S(1)}, u32[]{:S(2)}, u32[]{:S(2)}) async-start(bf16[32,9,8,128]{3,2,1,0:T(8,128)(2,1)} %bitcast.2), calls=%async_computation.1 | async-start | bytes 1179648 | tf_op jit(solution)/shard_map/all_to_all | solution.py:243
  27.4 0.2 collective-permute-start.3
  27.6 16.6 %all-to-all-done.1.parts_ref = bf16[32,9,8,128]{3,2,1,0:T(8,128)(2,1)S(1)} async-done(((bf16[32,9,8,128]{3,2,1,0:T(8,128)(2,1)}), bf16[32,9,8,128]{3,2,1,0:T(8,128)(2,1)S(1)}, u32[]{:S(2)}, u32[]{:S(2)}) %all-to-all-start.1) | async-done | bytes 589856 | tf_op jit(solution)/shard_map/all_to_all | solution.py:243
  44.2 0.0 copy-done.3
  44.2 0.5 %totals.1 = (bf16[128,32]{1,0:T(8,128)(2,1)S(1)}, f32[32,128]{1,0:T(8,128)S(1)}, f32[1,32]{1,0:T(1,128)S(1)}, f32[1,32]{1,0:T(1,128)S(1)}) custom-call(bf16[32,9,8,128]{3,2,1,0:T(8,128)(2,1)S(1)} %all-to-all-done.1.parts_ref, f32[128,32]{1,0:T(8,128)S(1)} %get-tuple-element.15.logits_ref, s32[1,32]{1,0:T(1,128)S(1)} %bitcast.13, s32[1,32]{1,0:T(1,128)S(1)} %bitcast.10), custom_call_target="tpu_custom_call" | custom-call | flops 32768 | bytes 65536 | tf_op jit(solution)/shard_map/totals/pallas_call | solution.py:247
  44.7 0.0 collective-permute-done.3.other_ref
  44.7 2.2 %finish.1 = (bf16[128,8192]{1,0:T(8,128)(2,1)}, f32[8,1024]{1,0:T(8,128)}, f32[1,1]{1,0:T(1,128)}, f32[1,1]{1,0:T(1,128)}) custom-call(bf16[128,32]{1,0:T(8,128)(2,1)S(1)} %get-tuple-element.16.dlogits_ref, bf16[4,8,8,512]{3,2,1,0:T(8,128)(2,1)S(1)} %bitcast.9, bf16[4,8,8,512]{3,2,1,0:T(8,128)(2,1)S(1)} %collective-permute-done.3.other_ref, ...), custom_call_target="tpu_custom_call" | custom-call | flops 67108864 | bytes 2621440 | tf_op jit(solution)/shard_map/finish/pallas_call | solution.py:266
  (1 shorter events, 0.0 us)
Async XLA Ops:
  0.6 20.7 %collective-permute-start = (bf16[128,8192]{1,0:T(8,128)(2,1)}, bf16[128,8192]{1,0:T(8,128)(2,1)S(1)}, u32[]{:S(2)}, u32[]{:S(2)}) collective-permute-start(bf16[128,8192]{1,0:T(8,128)(2,1)} %own_ref.1), channel_id=1, source_target_pairs={{0,1},{1,0},{2,3},{3,2},{4,5},{5,4},{6,7},{7,6},{8,9},{9,8},{10,11... | collective-permute-start | bytes 6291464 | tf_op jit(solution)/shard_map/ppermute | solution.py:202
  1.2 0.7 %copy-start.2 = (bf16[8,1024]{1,0:T(8,128)(2,1)S(1)}, bf16[8,1024]{1,0:T(8,128)(2,1)}, u32[]{:S(2)}) copy-start(bf16[8,1024]{1,0:T(8,128)(2,1)} %hidden_ref.1) | copy-start | bytes 49156
  19.3 1.6 %copy-start = (bf16[128,8192]{1,0:T(8,128)(2,1)S(1)}, bf16[128,8192]{1,0:T(8,128)(2,1)}, u32[]{:S(2)}) copy-start(bf16[128,8192]{1,0:T(8,128)(2,1)} %own_ref.1) | copy-start | bytes 6291460
  20.8 2.4 %copy-start.1 = (bf16[128,8192]{1,0:T(8,128)(2,1)S(1)}, bf16[128,8192]{1,0:T(8,128)(2,1)}, u32[]{:S(2)}) copy-start(bf16[128,8192]{1,0:T(8,128)(2,1)} %own_ref.1) | copy-start | bytes 6291460
  20.8 2.4 %copy-start.4 = (s32[32]{0:T(128)S(1)}, s32[32]{0:T(128)}, u32[]{:S(2)}) copy-start(s32[32]{0:T(128)} %param.6) | copy-start | bytes 388
  21.3 1.3 %collective-permute-start.2 = (f32[128,32]{1,0:T(8,128)S(1)}, f32[128,32]{1,0:T(8,128)S(1)}, u32[]{:S(2)}, u32[]{:S(2)}) collective-permute-start(f32[128,32]{1,0:T(8,128)S(1)} %half_logits.2.own_mine_ref), channel_id=1, source_target_pairs={{0,1},{1,0},{2,3},{3,2},{4,5},{5,4},{6,7},{7,6},{8,9},{9,8},{10,11... | collective-permute-start | bytes 49160 | tf_op jit(solution)/shard_map/ppermute | solution.py:226
  21.8 1.5 %collective-permute-start.1 = (f32[128,32]{1,0:T(8,128)S(1)}, f32[128,32]{1,0:T(8,128)S(1)}, u32[]{:S(2)}, u32[]{:S(2)}) collective-permute-start(f32[128,32]{1,0:T(8,128)S(1)} %half_logits.3.pair_mine_ref), channel_id=1, source_target_pairs={{0,1},{1,0},{2,3},{3,2},{4,5},{5,4},{6,7},{7,6},{8,9},{9,8},{10,11... | collective-permute-start | bytes 49160 | tf_op jit(solution)/shard_map/ppermute | solution.py:224
  23.2 20.9 %copy-start.3 = (s32[32]{0:T(128)S(1)}, s32[32]{0:T(128)}, u32[]{:S(2)}) copy-start(s32[32]{0:T(128)} %param.7) | copy-start | bytes 388
  24.8 19.4 %all-to-all-start.1 = ((bf16[32,9,8,128]{3,2,1,0:T(8,128)(2,1)}), bf16[32,9,8,128]{3,2,1,0:T(8,128)(2,1)S(1)}, u32[]{:S(2)}, u32[]{:S(2)}) async-start(bf16[32,9,8,128]{3,2,1,0:T(8,128)(2,1)} %bitcast.2), calls=%async_computation.1 | async-start | bytes 1179648 | tf_op jit(solution)/shard_map/all_to_all | solution.py:243
  27.4 17.3 %collective-permute-start.3 = (bf16[4,8,8,512]{3,2,1,0:T(8,128)(2,1)S(1)}, bf16[4,8,8,512]{3,2,1,0:T(8,128)(2,1)S(1)}, u32[]{:S(2)}, u32[]{:S(2)}) collective-permute-start(bf16[4,8,8,512]{3,2,1,0:T(8,128)(2,1)S(1)} %bitcast.8), channel_id=1, source_target_pairs={{0,1},{1,0},{2,3},{3,2},{4,5},{5,4},{6,7},{7,6},{8,9},{9,8},{10,11... | collective-permute-start | bytes 786440 | tf_op jit(solution)/shard_map/ppermute | solution.py:227

commit v6 on v5

--- a/solution.py
+++ b/solution.py
@@ -148,6 +148,9 @@
     ce_ref,
     z_ref,
     blocks_ref,
+    shares_ref,
+    losses_ref,
+    block_sems,
     sems,
 ):
     sections, tensors, rows, half = mine_ref.shape
@@ -155,8 +158,32 @@
     chips = sections * tensors // 2
     pieces = half // LANES
     core = this_core()
+    copies = []
+
+    def send(source, target, sem):
+        copies.append(pltpu.make_async_copy(source, target, sem))
+        copies[-1].start()
+
+    log_total = log_total_ref[...]
+    kept = mask_ref[...].astype(F32)
+    losses_ref[0] = jnp.sum(kept * (log_total - picked_ref[...]), axis=1, keepdims=True) / tokens
+    losses_ref[1] = jnp.sum(kept * log_total * log_total, axis=1, keepdims=True) / tokens
+    send(losses_ref.at[0], ce_ref, sems.at[0])
+    send(losses_ref.at[1], z_ref, sems.at[1])
+
+    here = scales_ref[pl.ds(pl.multiple_of(lax.axis_index("section") * rows, rows), rows), :]
+
+    def share(part, j):
+        weighted = jnp.zeros((rows, LANES), F32)
+        targeted = jnp.zeros((rows, LANES), F32)
+        for k in range(chips):
+            weighted += here[:, k : k + 1] * parts_ref[2 * k + part, j].astype(F32)
+            targeted += parts_ref[2 * k + part, pieces + j].astype(F32)
+        start = part * half + j * LANES
+        shares_ref[:, start : start + LANES] = weighted + here[:, chips : chips + 1] * targeted
+
     dlogits = dlogits_ref[...]
-    copies = []
+    tasks = [(part, j) for part in range(2) for j in range(pieces)]
     for t in range(tensors):
         for ref, place in ((mine_ref, core), (other_ref, 1 - core)):
             x = ref[:, t].reshape(tokens, half)
@@ -164,24 +191,11 @@
                 dlogits, x, preferred_element_type=F32
             ).astype(BF16)
         columns = slice(2 * t * half, 2 * (t + 1) * half)
-        copies.append(pltpu.make_async_copy(blocks_ref.at[:, columns], weight_grad_ref.at[:, columns], sems.at[t]))
-        copies[-1].start()
-
-    here = scales_ref[pl.ds(pl.multiple_of(lax.axis_index("section") * rows, rows), rows), :]
-    for part in range(2):
-        for j in range(pieces):
-            weighted = jnp.zeros((rows, LANES), F32)
-            targeted = jnp.zeros((rows, LANES), F32)
-            for k in range(chips):
-                weighted += here[:, k : k + 1] * parts_ref[2 * k + part, j].astype(F32)
-                targeted += parts_ref[2 * k + part, pieces + j].astype(F32)
-            start = part * half + j * LANES
-            hidden_grad_ref[:, start : start + LANES] = weighted + here[:, chips : chips + 1] * targeted
-
-    log_total = log_total_ref[...]
-    kept = mask_ref[...].astype(F32)
-    ce_ref[...] = jnp.sum(kept * (log_total - picked_ref[...]), axis=1, keepdims=True) / tokens
-    z_ref[...] = jnp.sum(kept * log_total * log_total, axis=1, keepdims=True) / tokens
+        send(blocks_ref.at[:, columns], weight_grad_ref.at[:, columns], block_sems.at[t])
+        for _ in range(min(len(tasks), -(-2 * pieces // max(tensors - 2, 1)))):
+            share(*tasks.pop(0))
+            if not tasks:
+                send(shares_ref, hidden_grad_ref, sems.at[2])
     for copy in copies:
         copy.wait()
 
@@ -272,8 +286,14 @@
             scalar,
         ),
         in_specs=[VMEM] * 8,
-        out_specs=(HBM, VMEM, VMEM, VMEM),
-        scratch_shapes=[pltpu.VMEM((vocab_dev, width), BF16), DMA((tensors,))],
+        out_specs=(HBM,) * 4,
+        scratch_shapes=[
+            pltpu.VMEM((vocab_dev, width), BF16),
+            pltpu.VMEM((rows, block), F32),
+            pltpu.VMEM((2, 1, 1), F32),
+            DMA((tensors,)),
+            DMA((3,)),
+        ],
         compiler_params=SMALL,
         cost_estimate=pl.CostEstimate(
             flops=flops, bytes_accessed=2 * vocab_dev * width + 2 * tokens * width, transcendentals=0

time: 47.2 us -> 46.6 us (0.987)
  Pallas kernels: 5.09 us -> 4.51 us
    pallas_call x1, Pallas kernels: 2.21 us -> 1.63 us  [body(): pl.pallas_call(finish_kernel, out_shape=(jax.ShapeDtypeStruct((vocab_dev,...]
where the time goes in v6:
time: 46.6 us; the launch traced here: 46.3 us
  waiting for transfers between devices  17.5 us (38%)
  blocking collectives  17.3 us (37%)
  Pallas kernels  4.51 us (10%)
  starting transfers between devices  3.97 us (9%)
  local copies, waits for them, and re-layouts  2.32 us (5%)
  between operations  0.68 us (1%)
    all_to_all x1, blocking collectives, body(): mine = lax.all_to_all(sent, BOTH, 0, 0)  17.3 us
    all_to_all x1, waiting for transfers between devices, body(): lax.all_to_all(parts.reshape(devices, tiles, rows, LANES), BOTH, 0, 0)  16.6 us
    all_to_all x1, starting transfers between devices, body(): lax.all_to_all(parts.reshape(devices, tiles, rows, LANES), BOTH, 0, 0)  2.61 us
    unnamed x10, local copies, waits for them, and re-layouts  2.32 us
    pallas_call x1, Pallas kernels, body(): pl.pallas_call(finish_kernel, out_shape=(jax.ShapeDtypeStruct((vocab_dev,...  1.63 us
    pallas_call x1, Pallas kernels, body(): pl.pallas_call(parts_kernel, out_shape=(jax.ShapeDtypeStruct((vocab_dev,...  1.5 us
  transfers between devices with their start and end apart: 5, of which 3 were waited for; matrix products, arithmetic and copies ran while one was open for 0% of the time, Pallas kernels for 3%

profile of v6, /device:TPU:0, one launch (start us, length us, event | category | flops | bytes accessed | tf_op | source)
XLA Modules:
  0.0 46.3 jit_solution(335714288213377915)
XLA Ops:
  0.6 0.6 %collective-permute-start = (bf16[128,8192]{1,0:T(8,128)(2,1)}, bf16[128,8192]{1,0:T(8,128)(2,1)S(1)}, u32[]{:S(2)}, u32[]{:S(2)}) collective-permute-start(bf16[128,8192]{1,0:T(8,128)(2,1)} %own_ref.1), channel_id=1, source_target_pairs={{0,1},{1,0},{2,3},{3,2},{4,5},{5,4},{6,7},{7,6},{8,9},{9,8},{10,11... | collective-permute-start | bytes 6291464 | tf_op jit(solution)/shard_map/ppermute | solution.py:216
  1.2 0.0 copy-start.2
  1.2 0.7 %copy-done.2 = bf16[8,1024]{1,0:T(8,128)(2,1)S(1)} copy-done((bf16[8,1024]{1,0:T(8,128)(2,1)S(1)}, bf16[8,1024]{1,0:T(8,128)(2,1)}, u32[]{:S(2)}) %copy-start.2) | copy-done | bytes 16408
  1.9 17.3 %all_to_all.10 = bf16[32,8,512]{2,1,0:T(8,128)(2,1)S(1)} all-to-all(bf16[32,8,512]{2,1,0:T(8,128)(2,1)S(1)} %spread_rows.1), channel_id=1, replica_groups=mesh['section'=4,'tensor'=8] {'section','tensor'}, dimensions={0} | all-to-all | bytes 524288 | tf_op jit(solution)/shard_map/all_to_all | solution.py:225
  19.3 0.0 copy-start
  19.3 1.6 %copy-done = bf16[128,8192]{1,0:T(8,128)(2,1)S(1)} copy-done((bf16[128,8192]{1,0:T(8,128)(2,1)S(1)}, bf16[128,8192]{1,0:T(8,128)(2,1)}, u32[]{:S(2)}) %copy-start) | copy-done | bytes 2097176
  20.8 0.0 copy-start.1
  20.8 0.0 copy-start.4
  20.9 0.4 half_logits.2.own_mine_ref
  21.3 0.1 collective-permute-start.2
  21.3 0.0 collective-permute-done.weight_ref.pair_ref
  21.4 0.4 half_logits.3.pair_mine_ref
  21.8 0.6 %collective-permute-start.1 = (f32[128,32]{1,0:T(8,128)S(1)}, f32[128,32]{1,0:T(8,128)S(1)}, u32[]{:S(2)}, u32[]{:S(2)}) collective-permute-start(f32[128,32]{1,0:T(8,128)S(1)} %half_logits.3.pair_mine_ref), channel_id=1, source_target_pairs={{0,1},{1,0},{2,3},{3,2},{4,5},{5,4},{6,7},{7,6},{8,9},{9,8},{10,11... | collective-permute-start | bytes 49160 | tf_op jit(solution)/shard_map/ppermute | solution.py:238
  22.3 0.2 collective-permute-done.2.pair_other_ref
  22.6 0.7 %collective-permute-done.1.own_other_ref = f32[128,32]{1,0:T(8,128)S(1)} collective-permute-done((f32[128,32]{1,0:T(8,128)S(1)}, f32[128,32]{1,0:T(8,128)S(1)}, u32[]{:S(2)}, u32[]{:S(2)}) %collective-permute-start.1) | collective-permute-done | bytes 16416 | tf_op jit(solution)/shard_map/ppermute | solution.py:238
  23.2 0.0 copy-done.1
  23.2 0.0 copy-done.4
  23.2 0.0 copy-start.3
  23.2 1.5 %grad_parts.1 = (f32[128,32]{1,0:T(8,128)S(1)}, bf16[4,8,9,8,128]{4,3,2,1,0:T(8,128)(2,1)}) custom-call(f32[128,32]{1,0:T(8,128)S(1)} %half_logits.2.own_mine_ref, f32[128,32]{1,0:T(8,128)S(1)} %collective-permute-done.1.own_other_ref, f32[128,32]{1,0:T(8,128)S(1)} %half_logits.3.pair_mine_ref, f32[128,32]{1,0:T(8,128)S(1)} %collective-permute-done.2.pair_other_ref, ...), custom_call_target="tpu_custom_call" | custom-call | flops 201326592 | bytes 2097152 | tf_op jit(solution)/shard_map/grad_parts/pallas_call | solution.py:243
  24.8 2.6 %all-to-all-start.1 = ((bf16[32,9,8,128]{3,2,1,0:T(8,128)(2,1)}), bf16[32,9,8,128]{3,2,1,0:T(8,128)(2,1)S(1)}, u32[]{:S(2)}, u32[]{:S(2)}) async-start(bf16[32,9,8,128]{3,2,1,0:T(8,128)(2,1)} %bitcast.2), calls=%async_computation.1 | async-start | bytes 1179648 | tf_op jit(solution)/shard_map/all_to_all | solution.py:257
  27.4 0.2 collective-permute-start.3
  27.6 16.6 %all-to-all-done.1.parts_ref = bf16[32,9,8,128]{3,2,1,0:T(8,128)(2,1)S(1)} async-done(((bf16[32,9,8,128]{3,2,1,0:T(8,128)(2,1)}), bf16[32,9,8,128]{3,2,1,0:T(8,128)(2,1)S(1)}, u32[]{:S(2)}, u32[]{:S(2)}) %all-to-all-start.1) | async-done | bytes 589856 | tf_op jit(solution)/shard_map/all_to_all | solution.py:257
  44.2 0.0 copy-done.3
  44.2 0.5 %totals.1 = (bf16[128,32]{1,0:T(8,128)(2,1)S(1)}, f32[32,128]{1,0:T(8,128)S(1)}, f32[1,32]{1,0:T(1,128)S(1)}, f32[1,32]{1,0:T(1,128)S(1)}) custom-call(bf16[32,9,8,128]{3,2,1,0:T(8,128)(2,1)S(1)} %all-to-all-done.1.parts_ref, f32[128,32]{1,0:T(8,128)S(1)} %get-tuple-element.15.logits_ref, s32[1,32]{1,0:T(1,128)S(1)} %bitcast.13, s32[1,32]{1,0:T(1,128)S(1)} %bitcast.10), custom_call_target="tpu_custom_call" | custom-call | flops 32768 | bytes 65536 | tf_op jit(solution)/shard_map/totals/pallas_call | solution.py:261
  44.7 0.0 collective-permute-done.3.other_ref
  44.7 1.6 %finish.1 = (bf16[128,8192]{1,0:T(8,128)(2,1)}, f32[8,1024]{1,0:T(8,128)}, f32[1,1]{1,0:T(1,128)}, f32[1,1]{1,0:T(1,128)}) custom-call(bf16[128,32]{1,0:T(8,128)(2,1)S(1)} %get-tuple-element.16.dlogits_ref, bf16[4,8,8,512]{3,2,1,0:T(8,128)(2,1)S(1)} %bitcast.9, bf16[4,8,8,512]{3,2,1,0:T(8,128)(2,1)S(1)} %collective-permute-done.3.other_ref, ...), custom_call_target="tpu_custom_call" | custom-call | flops 67108864 | bytes 2621440 | tf_op jit(solution)/shard_map/finish/pallas_call | solution.py:280
  (1 shorter events, 0.0 us)
Async XLA Ops:
  0.6 20.7 %collective-permute-start = (bf16[128,8192]{1,0:T(8,128)(2,1)}, bf16[128,8192]{1,0:T(8,128)(2,1)S(1)}, u32[]{:S(2)}, u32[]{:S(2)}) collective-permute-start(bf16[128,8192]{1,0:T(8,128)(2,1)} %own_ref.1), channel_id=1, source_target_pairs={{0,1},{1,0},{2,3},{3,2},{4,5},{5,4},{6,7},{7,6},{8,9},{9,8},{10,11... | collective-permute-start | bytes 6291464 | tf_op jit(solution)/shard_map/ppermute | solution.py:216
  1.2 0.7 %copy-start.2 = (bf16[8,1024]{1,0:T(8,128)(2,1)S(1)}, bf16[8,1024]{1,0:T(8,128)(2,1)}, u32[]{:S(2)}) copy-start(bf16[8,1024]{1,0:T(8,128)(2,1)} %hidden_ref.1) | copy-start | bytes 49156
  19.3 1.6 %copy-start = (bf16[128,8192]{1,0:T(8,128)(2,1)S(1)}, bf16[128,8192]{1,0:T(8,128)(2,1)}, u32[]{:S(2)}) copy-start(bf16[128,8192]{1,0:T(8,128)(2,1)} %own_ref.1) | copy-start | bytes 6291460
  20.8 2.4 %copy-start.1 = (bf16[128,8192]{1,0:T(8,128)(2,1)S(1)}, bf16[128,8192]{1,0:T(8,128)(2,1)}, u32[]{:S(2)}) copy-start(bf16[128,8192]{1,0:T(8,128)(2,1)} %own_ref.1) | copy-start | bytes 6291460
  20.8 2.4 %copy-start.4 = (s32[32]{0:T(128)S(1)}, s32[32]{0:T(128)}, u32[]{:S(2)}) copy-start(s32[32]{0:T(128)} %param.6) | copy-start | bytes 388
  21.3 1.3 %collective-permute-start.2 = (f32[128,32]{1,0:T(8,128)S(1)}, f32[128,32]{1,0:T(8,128)S(1)}, u32[]{:S(2)}, u32[]{:S(2)}) collective-permute-start(f32[128,32]{1,0:T(8,128)S(1)} %half_logits.2.own_mine_ref), channel_id=1, source_target_pairs={{0,1},{1,0},{2,3},{3,2},{4,5},{5,4},{6,7},{7,6},{8,9},{9,8},{10,11... | collective-permute-start | bytes 49160 | tf_op jit(solution)/shard_map/ppermute | solution.py:240
  21.8 1.5 %collective-permute-start.1 = (f32[128,32]{1,0:T(8,128)S(1)}, f32[128,32]{1,0:T(8,128)S(1)}, u32[]{:S(2)}, u32[]{:S(2)}) collective-permute-start(f32[128,32]{1,0:T(8,128)S(1)} %half_logits.3.pair_mine_ref), channel_id=1, source_target_pairs={{0,1},{1,0},{2,3},{3,2},{4,5},{5,4},{6,7},{7,6},{8,9},{9,8},{10,11... | collective-permute-start | bytes 49160 | tf_op jit(solution)/shard_map/ppermute | solution.py:238
  23.2 20.9 %copy-start.3 = (s32[32]{0:T(128)S(1)}, s32[32]{0:T(128)}, u32[]{:S(2)}) copy-start(s32[32]{0:T(128)} %param.7) | copy-start | bytes 388
  24.8 19.4 %all-to-all-start.1 = ((bf16[32,9,8,128]{3,2,1,0:T(8,128)(2,1)}), bf16[32,9,8,128]{3,2,1,0:T(8,128)(2,1)S(1)}, u32[]{:S(2)}, u32[]{:S(2)}) async-start(bf16[32,9,8,128]{3,2,1,0:T(8,128)(2,1)} %bitcast.2), calls=%async_computation.1 | async-start | bytes 1179648 | tf_op jit(solution)/shard_map/all_to_all | solution.py:257
  27.4 17.3 %collective-permute-start.3 = (bf16[4,8,8,512]{3,2,1,0:T(8,128)(2,1)S(1)}, bf16[4,8,8,512]{3,2,1,0:T(8,128)(2,1)S(1)}, u32[]{:S(2)}, u32[]{:S(2)}) collective-permute-start(bf16[4,8,8,512]{3,2,1,0:T(8,128)(2,1)S(1)} %bitcast.8), channel_id=1, source_target_pairs={{0,1},{1,0},{2,3},{3,2},{4,5},{5,4},{6,7},{7,6},{8,9},{9,8},{10,11... | collective-permute-start | bytes 786440 | tf_op jit(solution)/shard_map/ppermute | solution.py:241

commit v7 on v6

--- a/solution.py
+++ b/solution.py
@@ -9,6 +9,7 @@
 z_weight = 0.0001
 BOTH = ("section", "tensor")
 LANES = 128
+SUB = 4
 VMEM = pl.BlockSpec(memory_space=pltpu.VMEM)
 HBM = pl.BlockSpec(memory_space=pltpu.HBM)
 DMA = pltpu.SemaphoreType.DMA
@@ -58,9 +59,11 @@
     own_mine_ref, own_other_ref, pair_mine_ref, pair_other_ref, targets_ref, own_ref, pair_ref, logits_ref, out_ref
 ):
     vocab_dev, tokens = own_mine_ref.shape
-    sections, tensors, _, rows, _ = out_ref.shape
+    sections, tensors = out_ref.shape[:2]
+    rows = tokens // sections
     half = own_ref.shape[1] // tensors // 2
     pieces = half // LANES
+    first = 2 * pieces * (rows // SUB)
     core = this_core()
     targets = targets_ref[...]
     logits = (own_mine_ref[...] + own_other_ref[...], pair_mine_ref[...] + pair_other_ref[...])
@@ -86,8 +89,11 @@
         targeted = part[2 * tokens :].reshape(sections, rows, half).astype(BF16)
         for j in range(pieces):
             lanes = slice(j * LANES, (j + 1) * LANES)
-            out_ref[:, t, j] = weighted[:, :, lanes]
-            out_ref[:, t, pieces + j] = targeted[:, :, lanes]
+            for i in range(rows // SUB):
+                some = slice(i * SUB, (i + 1) * SUB)
+                tile = j * (rows // SUB) + i
+                out_ref[:, t, tile] = weighted[:, some, lanes]
+                out_ref[:, t, first // 2 + tile] = targeted[:, some, lanes]
 
     spare = tiles_of(3 * tokens) * LANES - 3 * tokens
     row = [top, total, picked] + ([jnp.zeros((1, spare), F32)] if spare else [])
@@ -96,12 +102,12 @@
     for _ in range(3):
         digits.append(row.astype(BF16).astype(F32))
         row = row - digits[-1]
-    digits.append(jnp.zeros((rows - 3, row.shape[1]), F32))
+    digits.append(jnp.zeros((SUB - 3, row.shape[1]), F32))
     digits = jnp.concatenate(digits, axis=0).astype(BF16)
     for j in range(tiles_of(3 * tokens)):
         tile = digits[:, j * LANES : (j + 1) * LANES]
         for t in range(tensors):
-            out_ref[:, t, 2 * pieces + j] = jnp.broadcast_to(tile[None], (sections, rows, LANES))
+            out_ref[:, t, first + j] = jnp.broadcast_to(tile[None], (sections, SUB, LANES))
 
 
 def totals_kernel(
@@ -174,13 +180,16 @@
     here = scales_ref[pl.ds(pl.multiple_of(lax.axis_index("section") * rows, rows), rows), :]
 
     def share(part, j):
-        weighted = jnp.zeros((rows, LANES), F32)
-        targeted = jnp.zeros((rows, LANES), F32)
-        for k in range(chips):
-            weighted += here[:, k : k + 1] * parts_ref[2 * k + part, j].astype(F32)
-            targeted += parts_ref[2 * k + part, pieces + j].astype(F32)
-        start = part * half + j * LANES
-        shares_ref[:, start : start + LANES] = weighted + here[:, chips : chips + 1] * targeted
+        for i in range(rows // SUB):
+            some = slice(i * SUB, (i + 1) * SUB)
+            tile = j * (rows // SUB) + i
+            weighted = jnp.zeros((SUB, LANES), F32)
+            targeted = jnp.zeros((SUB, LANES), F32)
+            for k in range(chips):
+                weighted += here[some, k : k + 1] * parts_ref[2 * k + part, tile].astype(F32)
+                targeted += parts_ref[2 * k + part, pieces * (rows // SUB) + tile].astype(F32)
+            start = part * half + j * LANES
+            shares_ref[some, start : start + LANES] = weighted + here[some, chips : chips + 1] * targeted
 
     dlogits = dlogits_ref[...]
     tasks = [(part, j) for part in range(2) for j in range(pieces)]
@@ -211,7 +220,7 @@
     target_row = targets.reshape(1, tokens)
     mask_row = token_mask.reshape(1, tokens)
     flops = 2 * tokens * vocab_dev * width
-    tiles = 2 * (half // LANES) + tiles_of(3 * tokens)
+    tiles = 2 * (half // LANES) * (rows // SUB) + tiles_of(3 * tokens)
 
     pair_weight = lax.ppermute(out_weight, "tensor", swap)
     sent = pl.pallas_call(
@@ -244,7 +253,7 @@
         parts_kernel,
         out_shape=(
             jax.ShapeDtypeStruct((vocab_dev, tokens), F32),
-            jax.ShapeDtypeStruct((sections, tensors, tiles, rows, LANES), BF16),
+            jax.ShapeDtypeStruct((sections, tensors, tiles, SUB, LANES), BF16),
         ),
         in_specs=[VMEM] * 7,
         out_specs=(VMEM, VMEM),
@@ -254,7 +263,7 @@
         ),
         name="grad_parts",
     )(own_mine, own_other, pair_mine, pair_other, target_row, out_weight, pair_weight)
-    parts = lax.all_to_all(parts.reshape(devices, tiles, rows, LANES), BOTH, 0, 0)
+    parts = lax.all_to_all(parts.reshape(devices, tiles, SUB, LANES), BOTH, 0, 0)
 
     chips = devices // 2
     row = jax.ShapeDtypeStruct((1, tokens), F32)

time: 46.6 us -> 46 us (0.987)
  waiting for transfers between devices: 17.5 us -> 16.9 us
    all_to_all x1, waiting for transfers between devices: 16.6 us -> 16 us  [body(): lax.all_to_all(parts.reshape(devices, tiles, SUB, LANES), BOTH, 0, 0)]
where the time goes in v7:
time: 46 us; the launch traced here: 45.7 us
  blocking collectives  17.3 us (38%)
  waiting for transfers between devices  16.9 us (37%)
  Pallas kernels  4.52 us (10%)
  starting transfers between devices  3.97 us (9%)
  local copies, waits for them, and re-layouts  2.32 us (5%)
  between operations  0.68 us (1%)
    all_to_all x1, blocking collectives, body(): mine = lax.all_to_all(sent, BOTH, 0, 0)  17.3 us
    all_to_all x1, waiting for transfers between devices, body(): lax.all_to_all(parts.reshape(devices, tiles, SUB, LANES), BOTH, 0, 0)  16 us
    all_to_all x1, starting transfers between devices, body(): lax.all_to_all(parts.reshape(devices, tiles, SUB, LANES), BOTH, 0, 0)  2.61 us
    unnamed x10, local copies, waits for them, and re-layouts  2.32 us
    pallas_call x1, Pallas kernels, body(): pl.pallas_call(finish_kernel, out_shape=(jax.ShapeDtypeStruct((vocab_dev,...  1.63 us
    pallas_call x1, Pallas kernels, body(): pl.pallas_call(parts_kernel, out_shape=(jax.ShapeDtypeStruct((vocab_dev,...  1.5 us
  transfers between devices with their start and end apart: 5, of which 3 were waited for; matrix products, arithmetic and copies ran while one was open for 0% of the time, Pallas kernels for 3%

profile of v7, /device:TPU:0, one launch (start us, length us, event | category | flops | bytes accessed | tf_op | source)
XLA Modules:
  0.0 45.7 jit_solution(16606039508538398562)
XLA Ops:
  0.6 0.6 %collective-permute-start = (bf16[128,8192]{1,0:T(8,128)(2,1)}, bf16[128,8192]{1,0:T(8,128)(2,1)S(1)}, u32[]{:S(2)}, u32[]{:S(2)}) collective-permute-start(bf16[128,8192]{1,0:T(8,128)(2,1)} %own_ref.1), channel_id=1, source_target_pairs={{0,1},{1,0},{2,3},{3,2},{4,5},{5,4},{6,7},{7,6},{8,9},{9,8},{10,11... | collective-permute-start | bytes 6291464 | tf_op jit(solution)/shard_map/ppermute | solution.py:225
  1.2 0.0 copy-start.2
  1.2 0.7 %copy-done.2 = bf16[8,1024]{1,0:T(8,128)(2,1)S(1)} copy-done((bf16[8,1024]{1,0:T(8,128)(2,1)S(1)}, bf16[8,1024]{1,0:T(8,128)(2,1)}, u32[]{:S(2)}) %copy-start.2) | copy-done | bytes 16408
  1.9 17.3 %all_to_all.10 = bf16[32,8,512]{2,1,0:T(8,128)(2,1)S(1)} all-to-all(bf16[32,8,512]{2,1,0:T(8,128)(2,1)S(1)} %spread_rows.1), channel_id=1, replica_groups=mesh['section'=4,'tensor'=8] {'section','tensor'}, dimensions={0} | all-to-all | bytes 524288 | tf_op jit(solution)/shard_map/all_to_all | solution.py:234
  19.3 0.0 copy-start
  19.3 1.6 %copy-done = bf16[128,8192]{1,0:T(8,128)(2,1)S(1)} copy-done((bf16[128,8192]{1,0:T(8,128)(2,1)S(1)}, bf16[128,8192]{1,0:T(8,128)(2,1)}, u32[]{:S(2)}) %copy-start) | copy-done | bytes 2097176
  20.8 0.0 copy-start.1
  20.8 0.0 copy-start.3
  20.9 0.4 half_logits.2.own_mine_ref
  21.3 0.1 collective-permute-start.2
  21.3 0.0 collective-permute-done.weight_ref.pair_ref
  21.4 0.4 half_logits.3.pair_mine_ref
  21.8 0.6 %collective-permute-start.1 = (f32[128,32]{1,0:T(8,128)S(1)}, f32[128,32]{1,0:T(8,128)S(1)}, u32[]{:S(2)}, u32[]{:S(2)}) collective-permute-start(f32[128,32]{1,0:T(8,128)S(1)} %half_logits.3.pair_mine_ref), channel_id=1, source_target_pairs={{0,1},{1,0},{2,3},{3,2},{4,5},{5,4},{6,7},{7,6},{8,9},{9,8},{10,11... | collective-permute-start | bytes 49160 | tf_op jit(solution)/shard_map/ppermute | solution.py:247
  22.3 0.2 collective-permute-done.2.pair_other_ref
  22.6 0.7 %collective-permute-done.1.own_other_ref = f32[128,32]{1,0:T(8,128)S(1)} collective-permute-done((f32[128,32]{1,0:T(8,128)S(1)}, f32[128,32]{1,0:T(8,128)S(1)}, u32[]{:S(2)}, u32[]{:S(2)}) %collective-permute-start.1) | collective-permute-done | bytes 16416 | tf_op jit(solution)/shard_map/ppermute | solution.py:247
  23.2 0.0 copy-done.1
  23.2 0.0 copy-done.3
  23.2 0.0 copy-start.4
  23.2 1.5 %grad_parts.1 = (f32[128,32]{1,0:T(8,128)S(1)}, bf16[4,8,17,4,128]{4,3,2,1,0:T(4,128)(2,1)}) custom-call(f32[128,32]{1,0:T(8,128)S(1)} %half_logits.2.own_mine_ref, f32[128,32]{1,0:T(8,128)S(1)} %collective-permute-done.1.own_other_ref, f32[128,32]{1,0:T(8,128)S(1)} %half_logits.3.pair_mine_ref, f32[128,32]{1,0:T(8,128)S(1)} %collective-permute-done.2.pair_other_ref, ...), custom_call_target="tpu_custom_call" | custom-call | flops 201326592 | bytes 2097152 | tf_op jit(solution)/shard_map/grad_parts/pallas_call | solution.py:252
  24.8 2.6 %all-to-all-start.1 = ((bf16[32,17,4,128]{3,2,1,0:T(4,128)(2,1)}), bf16[32,17,4,128]{3,2,1,0:T(4,128)(2,1)S(1)}, u32[]{:S(2)}, u32[]{:S(2)}) async-start(bf16[32,17,4,128]{3,2,1,0:T(4,128)(2,1)} %bitcast.2), calls=%async_computation.1 | async-start | bytes 1114112 | tf_op jit(solution)/shard_map/all_to_all | solution.py:266
  27.4 0.2 collective-permute-start.3
  27.5 16.0 %all-to-all-done.1.parts_ref = bf16[32,17,4,128]{3,2,1,0:T(4,128)(2,1)S(1)} async-done(((bf16[32,17,4,128]{3,2,1,0:T(4,128)(2,1)}), bf16[32,17,4,128]{3,2,1,0:T(4,128)(2,1)S(1)}, u32[]{:S(2)}, u32[]{:S(2)}) %all-to-all-start.1) | async-done | bytes 557088 | tf_op jit(solution)/shard_map/all_to_all | solution.py:266
  43.6 0.0 copy-done.4
  43.6 0.5 %totals.1 = (bf16[128,32]{1,0:T(8,128)(2,1)S(1)}, f32[32,128]{1,0:T(8,128)S(1)}, f32[1,32]{1,0:T(1,128)S(1)}, f32[1,32]{1,0:T(1,128)S(1)}) custom-call(bf16[32,17,4,128]{3,2,1,0:T(4,128)(2,1)S(1)} %all-to-all-done.1.parts_ref, f32[128,32]{1,0:T(8,128)S(1)} %get-tuple-element.15.logits_ref, s32[1,32]{1,0:T(1,128)S(1)} %bitcast.11, s32[1,32]{1,0:T(1,128)S(1)} %bitcast.12), custom_call_target="tpu_custom_call" | custom-call | flops 32768 | bytes 65536 | tf_op jit(solution)/shard_map/totals/pallas_call | solution.py:270
  44.1 0.0 collective-permute-done.3.other_ref
  44.1 1.6 %finish.1 = (bf16[128,8192]{1,0:T(8,128)(2,1)}, f32[8,1024]{1,0:T(8,128)}, f32[1,1]{1,0:T(1,128)}, f32[1,1]{1,0:T(1,128)}) custom-call(bf16[128,32]{1,0:T(8,128)(2,1)S(1)} %get-tuple-element.16.dlogits_ref, bf16[4,8,8,512]{3,2,1,0:T(8,128)(2,1)S(1)} %bitcast.9, bf16[4,8,8,512]{3,2,1,0:T(8,128)(2,1)S(1)} %collective-permute-done.3.other_ref, ...), custom_call_target="tpu_custom_call" | custom-call | flops 67108864 | bytes 2621440 | tf_op jit(solution)/shard_map/finish/pallas_call | solution.py:289
  (1 shorter events, 0.0 us)
Async XLA Ops:
  0.6 20.7 %collective-permute-start = (bf16[128,8192]{1,0:T(8,128)(2,1)}, bf16[128,8192]{1,0:T(8,128)(2,1)S(1)}, u32[]{:S(2)}, u32[]{:S(2)}) collective-permute-start(bf16[128,8192]{1,0:T(8,128)(2,1)} %own_ref.1), channel_id=1, source_target_pairs={{0,1},{1,0},{2,3},{3,2},{4,5},{5,4},{6,7},{7,6},{8,9},{9,8},{10,11... | collective-permute-start | bytes 6291464 | tf_op jit(solution)/shard_map/ppermute | solution.py:225
  1.2 0.7 %copy-start.2 = (bf16[8,1024]{1,0:T(8,128)(2,1)S(1)}, bf16[8,1024]{1,0:T(8,128)(2,1)}, u32[]{:S(2)}) copy-start(bf16[8,1024]{1,0:T(8,128)(2,1)} %hidden_ref.1) | copy-start | bytes 49156
  19.3 1.6 %copy-start = (bf16[128,8192]{1,0:T(8,128)(2,1)S(1)}, bf16[128,8192]{1,0:T(8,128)(2,1)}, u32[]{:S(2)}) copy-start(bf16[128,8192]{1,0:T(8,128)(2,1)} %own_ref.1) | copy-start | bytes 6291460
  20.8 2.4 %copy-start.1 = (bf16[128,8192]{1,0:T(8,128)(2,1)S(1)}, bf16[128,8192]{1,0:T(8,128)(2,1)}, u32[]{:S(2)}) copy-start(bf16[128,8192]{1,0:T(8,128)(2,1)} %own_ref.1) | copy-start | bytes 6291460
  20.8 2.4 %copy-start.3 = (s32[32]{0:T(128)S(1)}, s32[32]{0:T(128)}, u32[]{:S(2)}) copy-start(s32[32]{0:T(128)} %param.6) | copy-start | bytes 388
  21.3 1.3 %collective-permute-start.2 = (f32[128,32]{1,0:T(8,128)S(1)}, f32[128,32]{1,0:T(8,128)S(1)}, u32[]{:S(2)}, u32[]{:S(2)}) collective-permute-start(f32[128,32]{1,0:T(8,128)S(1)} %half_logits.2.own_mine_ref), channel_id=1, source_target_pairs={{0,1},{1,0},{2,3},{3,2},{4,5},{5,4},{6,7},{7,6},{8,9},{9,8},{10,11... | collective-permute-start | bytes 49160 | tf_op jit(solution)/shard_map/ppermute | solution.py:249
  21.8 1.5 %collective-permute-start.1 = (f32[128,32]{1,0:T(8,128)S(1)}, f32[128,32]{1,0:T(8,128)S(1)}, u32[]{:S(2)}, u32[]{:S(2)}) collective-permute-start(f32[128,32]{1,0:T(8,128)S(1)} %half_logits.3.pair_mine_ref), channel_id=1, source_target_pairs={{0,1},{1,0},{2,3},{3,2},{4,5},{5,4},{6,7},{7,6},{8,9},{9,8},{10,11... | collective-permute-start | bytes 49160 | tf_op jit(solution)/shard_map/ppermute | solution.py:247
  23.2 20.3 %copy-start.4 = (s32[32]{0:T(128)S(1)}, s32[32]{0:T(128)}, u32[]{:S(2)}) copy-start(s32[32]{0:T(128)} %param.7) | copy-start | bytes 388
  24.8 18.8 %all-to-all-start.1 = ((bf16[32,17,4,128]{3,2,1,0:T(4,128)(2,1)}), bf16[32,17,4,128]{3,2,1,0:T(4,128)(2,1)S(1)}, u32[]{:S(2)}, u32[]{:S(2)}) async-start(bf16[32,17,4,128]{3,2,1,0:T(4,128)(2,1)} %bitcast.2), calls=%async_computation.1 | async-start | bytes 1114112 | tf_op jit(solution)/shard_map/all_to_all | solution.py:266
  27.4 16.7 %collective-permute-start.3 = (bf16[4,8,8,512]{3,2,1,0:T(8,128)(2,1)S(1)}, bf16[4,8,8,512]{3,2,1,0:T(8,128)(2,1)S(1)}, u32[]{:S(2)}, u32[]{:S(2)}) collective-permute-start(bf16[4,8,8,512]{3,2,1,0:T(8,128)(2,1)S(1)} %bitcast.8), channel_id=1, source_target_pairs={{0,1},{1,0},{2,3},{3,2},{4,5},{5,4},{6,7},{7,6},{8,9},{9,8},{10,11... | collective-permute-start | bytes 786440 | tf_op jit(solution)/shard_map/ppermute | solution.py:250

commit v8 on v7

--- a/solution.py
+++ b/solution.py
@@ -56,7 +56,7 @@
 
 
 def parts_kernel(
-    own_mine_ref, own_other_ref, pair_mine_ref, pair_other_ref, targets_ref, own_ref, pair_ref, logits_ref, out_ref
+    own_mine_ref, own_other_ref, pair_mine_ref, pair_other_ref, targets_ref, own_ref, pair_ref, _, logits_ref, out_ref
 ):
     vocab_dev, tokens = own_mine_ref.shape
     sections, tensors = out_ref.shape[:2]
@@ -110,11 +110,36 @@
             out_ref[:, t, first + j] = jnp.broadcast_to(tile[None], (sections, SUB, LANES))
 
 
-def totals_kernel(
-    parts_ref, logits_ref, targets_ref, mask_ref, dlogits_ref, scales_ref, log_total_ref, picked_ref, table_ref
+def finish_kernel(
+    parts_ref,
+    logits_ref,
+    targets_ref,
+    mask_ref,
+    mine_ref,
+    other_ref,
+    weight_grad_ref,
+    hidden_grad_ref,
+    ce_ref,
+    z_ref,
+    table_ref,
+    scales_ref,
+    blocks_ref,
+    shares_ref,
+    losses_ref,
+    block_sems,
+    sems,
 ):
-    chips = table_ref.shape[0]
-    tokens = log_total_ref.shape[1]
+    sections, tensors, rows, half = mine_ref.shape
+    tokens = sections * rows
+    chips = sections * tensors // 2
+    pieces = half // LANES
+    core = this_core()
+    copies = []
+
+    def send(source, target, sem):
+        copies.append(pltpu.make_async_copy(source, target, sem))
+        copies[-1].start()
+
     first = parts_ref.shape[1] - tiles_of(3 * tokens)
     for k in range(chips):
         for j in range(tiles_of(3 * tokens)):
@@ -130,49 +155,14 @@
     kept = mask_ref[...].astype(F32)
     factor = 1.0 + 2.0 * z_weight * log_total
     hit = target_hits(logits_ref.shape, targets_ref[...], False).astype(F32)
-    dlogits_ref[...] = (kept * (factor * jnp.exp(logits_ref[...] - log_total) - hit)).astype(BF16)
-    log_total_ref[...] = log_total
-    picked_ref[...] = picked
+    dlogits = (kept * (factor * jnp.exp(logits_ref[...] - log_total) - hit)).astype(BF16)
 
     scales = (kept * (factor * jnp.exp(tops - log_total))).astype(BF16).astype(F32)
     scale = (kept * (factor * jnp.exp(picked - log_total) - 1.0)).astype(BF16).astype(F32)
     spare = scales_ref.shape[1] - chips - 1
     scales_ref[...] = jnp.concatenate([scales, scale, jnp.zeros((spare, tokens), F32)], axis=0).T
 
-
-def finish_kernel(
-    dlogits_ref,
-    mine_ref,
-    other_ref,
-    parts_ref,
-    scales_ref,
-    log_total_ref,
-    picked_ref,
-    mask_ref,
-    weight_grad_ref,
-    hidden_grad_ref,
-    ce_ref,
-    z_ref,
-    blocks_ref,
-    shares_ref,
-    losses_ref,
-    block_sems,
-    sems,
-):
-    sections, tensors, rows, half = mine_ref.shape
-    tokens = sections * rows
-    chips = sections * tensors // 2
-    pieces = half // LANES
-    core = this_core()
-    copies = []
-
-    def send(source, target, sem):
-        copies.append(pltpu.make_async_copy(source, target, sem))
-        copies[-1].start()
-
-    log_total = log_total_ref[...]
-    kept = mask_ref[...].astype(F32)
-    losses_ref[0] = jnp.sum(kept * (log_total - picked_ref[...]), axis=1, keepdims=True) / tokens
+    losses_ref[0] = jnp.sum(kept * (log_total - picked), axis=1, keepdims=True) / tokens
     losses_ref[1] = jnp.sum(kept * log_total * log_total, axis=1, keepdims=True) / tokens
     send(losses_ref.at[0], ce_ref, sems.at[0])
     send(losses_ref.at[1], z_ref, sems.at[1])
@@ -191,7 +181,6 @@
             start = part * half + j * LANES
             shares_ref[some, start : start + LANES] = weighted + here[some, chips : chips + 1] * targeted
 
-    dlogits = dlogits_ref[...]
     tasks = [(part, j) for part in range(2) for j in range(pieces)]
     for t in range(tensors):
         for ref, place in ((mine_ref, core), (other_ref, 1 - core)):
@@ -255,36 +244,17 @@
             jax.ShapeDtypeStruct((vocab_dev, tokens), F32),
             jax.ShapeDtypeStruct((sections, tensors, tiles, SUB, LANES), BF16),
         ),
-        in_specs=[VMEM] * 7,
+        in_specs=[VMEM] * 7 + [pl.BlockSpec(memory_space=pl.ANY)],
         out_specs=(VMEM, VMEM),
         compiler_params=SMALL,
         cost_estimate=pl.CostEstimate(
             flops=3 * flops, bytes_accessed=2 * vocab_dev * width, transcendentals=2 * vocab_dev * tokens
         ),
         name="grad_parts",
-    )(own_mine, own_other, pair_mine, pair_other, target_row, out_weight, pair_weight)
+    )(own_mine, own_other, pair_mine, pair_other, target_row, out_weight, pair_weight, other)
     parts = lax.all_to_all(parts.reshape(devices, tiles, SUB, LANES), BOTH, 0, 0)
 
     chips = devices // 2
-    row = jax.ShapeDtypeStruct((1, tokens), F32)
-    dlogits, scales, log_total, picked = pl.pallas_call(
-        totals_kernel,
-        out_shape=(
-            jax.ShapeDtypeStruct((vocab_dev, tokens), BF16),
-            jax.ShapeDtypeStruct((tokens, tiles_of(chips + 1) * LANES), F32),
-            row,
-            row,
-        ),
-        in_specs=[VMEM] * 4,
-        out_specs=(VMEM,) * 4,
-        scratch_shapes=[pltpu.VMEM((chips, tiles_of(3 * tokens) * LANES), F32)],
-        compiler_params=SMALL,
-        cost_estimate=pl.CostEstimate(
-            flops=8 * vocab_dev * tokens, bytes_accessed=16 * vocab_dev * tokens, transcendentals=vocab_dev * tokens
-        ),
-        name="totals",
-    )(parts, logits, target_row, mask_row)
-
     scalar = jax.ShapeDtypeStruct((1, 1), F32)
     grad_weight, grad_hidden, ce_loss, z_loss = pl.pallas_call(
         finish_kernel,
@@ -294,9 +264,11 @@
             scalar,
             scalar,
         ),
-        in_specs=[VMEM] * 8,
+        in_specs=[VMEM] * 6,
         out_specs=(HBM,) * 4,
         scratch_shapes=[
+            pltpu.VMEM((chips, tiles_of(3 * tokens) * LANES), F32),
+            pltpu.VMEM((tokens, tiles_of(chips + 1) * LANES), F32),
             pltpu.VMEM((vocab_dev, width), BF16),
             pltpu.VMEM((rows, block), F32),
             pltpu.VMEM((2, 1, 1), F32),
@@ -308,7 +280,7 @@
             flops=flops, bytes_accessed=2 * vocab_dev * width + 2 * tokens * width, transcendentals=0
         ),
         name="finish",
-    )(dlogits, mine, other, parts, scales, log_total, picked, mask_row)
+    )(parts, logits, target_row, mask_row, mine, other)
     return (ce_loss.reshape(()), z_loss.reshape(()), grad_hidden, grad_weight)
 
 

time: 46 us -> 45 us (0.978)
  blocking collectives: 17.3 us -> 35.7 us
  waiting for transfers between devices: 16.9 us -> 1.23 us
  starting transfers between devices: 3.97 us -> 1.22 us
  Pallas kernels: 4.52 us -> 3.51 us
    all_to_all x0 -> x1, blocking collectives: none -> 18.4 us  [body(): lax.all_to_all(parts.reshape(devices, tiles, SUB, LANES), BOTH, 0, 0)]
    all_to_all x1 -> x0, waiting for transfers between devices: 16 us -> none  [body(): lax.all_to_all(parts.reshape(devices, tiles, SUB, LANES), BOTH, 0, 0)]
    all_to_all x1 -> x0, starting transfers between devices: 2.61 us -> none  [body(): lax.all_to_all(parts.reshape(devices, tiles, SUB, LANES), BOTH, 0, 0)]
    pallas_call x1, Pallas kernels: 1.5 us -> 0.7 us  [body(): pl.pallas_call(parts_kernel, out_shape=(jax.ShapeDtypeStruct((vocab_dev,...]
    pallas_call x1 -> x0, Pallas kernels: 0.53 us -> none  [body(): pl.pallas_call(totals_kernel, out_shape=(jax.ShapeDtypeStruct((vocab_dev,...]
    ppermute x1, starting transfers between devices: 0.07 us -> 0.57 us  [body(): pair_other = lax.ppermute(own_mine, 'tensor', swap)]
    ppermute x1, starting transfers between devices: 0.55 us -> 0.09 us  [body(): own_other = lax.ppermute(pair_mine, 'tensor', swap)]
  transfers between devices with their start and end apart: 5 -> 4, of which waited for: 3 -> 2; matrix products, arithmetic and copies ran while one was open for 0% -> 0% of each run, Pallas kernels for 3% -> 2%
where the time goes in v8:
time: 45 us; the launch traced here: 44.7 us
  blocking collectives  35.7 us (79%)
  Pallas kernels  3.51 us (8%)
  local copies, waits for them, and re-layouts  2.32 us (5%)
  waiting for transfers between devices  1.23 us (3%)
  starting transfers between devices  1.22 us (3%)
  between operations  0.67 us (1%)
    all_to_all x1, blocking collectives, body(): lax.all_to_all(parts.reshape(devices, tiles, SUB, LANES), BOTH, 0, 0)  18.4 us
    all_to_all x1, blocking collectives, body(): mine = lax.all_to_all(sent, BOTH, 0, 0)  17.3 us
    unnamed x10, local copies, waits for them, and re-layouts  2.32 us
    pallas_call x1, Pallas kernels, body(): pl.pallas_call(finish_kernel, out_shape=(jax.ShapeDtypeStruct((vocab_dev,...  1.96 us
  transfers between devices with their start and end apart: 4, of which 2 were waited for; matrix products, arithmetic and copies ran while one was open for 0% of the time, Pallas kernels for 2%

profile of v8, /device:TPU:0, one launch (start us, length us, event | category | flops | bytes accessed | tf_op | source)
XLA Modules:
  0.0 44.7 jit_solution(3125471693395045627)
XLA Ops:
  0.6 0.6 %collective-permute-start = (bf16[128,8192]{1,0:T(8,128)(2,1)}, bf16[128,8192]{1,0:T(8,128)(2,1)S(1)}, u32[]{:S(2)}, u32[]{:S(2)}) collective-permute-start(bf16[128,8192]{1,0:T(8,128)(2,1)} %own_ref.1), channel_id=1, source_target_pairs={{0,1},{1,0},{2,3},{3,2},{4,5},{5,4},{6,7},{7,6},{8,9},{9,8},{10,11... | collective-permute-start | bytes 6291464 | tf_op jit(solution)/shard_map/ppermute | solution.py:214
  1.2 0.0 copy-start.2
  1.2 0.7 %copy-done.2 = bf16[8,1024]{1,0:T(8,128)(2,1)S(1)} copy-done((bf16[8,1024]{1,0:T(8,128)(2,1)S(1)}, bf16[8,1024]{1,0:T(8,128)(2,1)}, u32[]{:S(2)}) %copy-start.2) | copy-done | bytes 16408
  1.9 17.3 %all_to_all.10 = bf16[32,8,512]{2,1,0:T(8,128)(2,1)S(1)} all-to-all(bf16[32,8,512]{2,1,0:T(8,128)(2,1)S(1)} %spread_rows.1), channel_id=1, replica_groups=mesh['section'=4,'tensor'=8] {'section','tensor'}, dimensions={0} | all-to-all | bytes 524288 | tf_op jit(solution)/shard_map/all_to_all | solution.py:223
  19.3 0.0 collective-permute-start.3
  19.3 0.0 copy-start
  19.3 1.6 %copy-done = bf16[128,8192]{1,0:T(8,128)(2,1)S(1)} copy-done((bf16[128,8192]{1,0:T(8,128)(2,1)S(1)}, bf16[128,8192]{1,0:T(8,128)(2,1)}, u32[]{:S(2)}) %copy-start) | copy-done | bytes 2097176
  20.9 0.0 copy-start.1
  20.9 0.0 copy-start.3
  20.9 0.4 half_logits.2.own_mine_ref
  21.3 0.6 %collective-permute-start.2 = (f32[128,32]{1,0:T(8,128)S(1)}, f32[128,32]{1,0:T(8,128)S(1)}, u32[]{:S(2)}, u32[]{:S(2)}) collective-permute-start(f32[128,32]{1,0:T(8,128)S(1)} %half_logits.2.own_mine_ref), channel_id=1, source_target_pairs={{0,1},{1,0},{2,3},{3,2},{4,5},{5,4},{6,7},{7,6},{8,9},{9,8},{10,11... | collective-permute-start | bytes 49160 | tf_op jit(solution)/shard_map/ppermute | solution.py:238
  21.9 0.0 collective-permute-done.weight_ref.pair_ref
  21.9 0.4 half_logits.3.pair_mine_ref
  22.3 0.1 collective-permute-start.1
  22.4 0.4 collective-permute-done.2.pair_other_ref
  22.8 0.0 collective-permute-done.3._.other_ref
  22.8 0.8 %collective-permute-done.1.own_other_ref = f32[128,32]{1,0:T(8,128)S(1)} collective-permute-done((f32[128,32]{1,0:T(8,128)S(1)}, f32[128,32]{1,0:T(8,128)S(1)}, u32[]{:S(2)}, u32[]{:S(2)}) %collective-permute-start.1) | collective-permute-done | bytes 16416 | tf_op jit(solution)/shard_map/ppermute | solution.py:236
  23.6 0.0 copy-done.1
  23.6 0.0 copy-done.3
  23.6 0.0 copy-start.4
  23.6 0.7 %grad_parts.1 = (f32[128,32]{1,0:T(8,128)S(1)}, bf16[4,8,17,4,128]{4,3,2,1,0:T(4,128)(2,1)S(1)}) custom-call(f32[128,32]{1,0:T(8,128)S(1)} %half_logits.2.own_mine_ref, f32[128,32]{1,0:T(8,128)S(1)} %collective-permute-done.1.own_other_ref, f32[128,32]{1,0:T(8,128)S(1)} %half_logits.3.pair_mine_ref, f32[128,32]{1,0:T(8,128)S(1)} %collective-permute-done.2.pair_other_ref, ...), custom_call_target="tpu_custom_call" | custom-call | flops 201326592 | bytes 2097152 | tf_op jit(solution)/shard_map/grad_parts/pallas_call | solution.py:241
  24.3 18.4 %all_to_all.11.parts_ref = bf16[32,17,4,128]{3,2,1,0:T(4,128)(2,1)S(1)} all-to-all(bf16[32,17,4,128]{3,2,1,0:T(4,128)(2,1)S(1)} %bitcast.10), channel_id=1, replica_groups=mesh['section'=4,'tensor'=8] {'section','tensor'}, dimensions={0} | all-to-all | bytes 1114112 | tf_op jit(solution)/shard_map/all_to_all | solution.py:255
  42.7 0.0 copy-done.4
  42.7 2.0 %finish.1 = (bf16[128,8192]{1,0:T(8,128)(2,1)}, f32[8,1024]{1,0:T(8,128)}, f32[1,1]{1,0:T(1,128)}, f32[1,1]{1,0:T(1,128)}) custom-call(bf16[32,17,4,128]{3,2,1,0:T(4,128)(2,1)S(1)} %all_to_all.11.parts_ref, f32[128,32]{1,0:T(8,128)S(1)} %get-tuple-element.11.logits_ref, s32[1,32]{1,0:T(1,128)S(1)} %bitcast.12, s32[1,32]{1,0:T(1,128)S(1)} %bitcast.13, ...), custom_call_target="tpu_custom_call" | custom-call | flops 67108864 | bytes 2621440 | tf_op jit(solution)/shard_map/finish/pallas_call | solution.py:259
  (1 shorter events, 0.0 us)
Async XLA Ops:
  0.6 21.2 %collective-permute-start = (bf16[128,8192]{1,0:T(8,128)(2,1)}, bf16[128,8192]{1,0:T(8,128)(2,1)S(1)}, u32[]{:S(2)}, u32[]{:S(2)}) collective-permute-start(bf16[128,8192]{1,0:T(8,128)(2,1)} %own_ref.1), channel_id=1, source_target_pairs={{0,1},{1,0},{2,3},{3,2},{4,5},{5,4},{6,7},{7,6},{8,9},{9,8},{10,11... | collective-permute-start | bytes 6291464 | tf_op jit(solution)/shard_map/ppermute | solution.py:214
  1.2 0.7 %copy-start.2 = (bf16[8,1024]{1,0:T(8,128)(2,1)S(1)}, bf16[8,1024]{1,0:T(8,128)(2,1)}, u32[]{:S(2)}) copy-start(bf16[8,1024]{1,0:T(8,128)(2,1)} %hidden_ref.1) | copy-start | bytes 49156
  19.3 3.5 %collective-permute-start.3 = (bf16[4,8,8,512]{3,2,1,0:T(8,128)(2,1)S(1)}, bf16[4,8,8,512]{3,2,1,0:T(8,128)(2,1)S(1)}, u32[]{:S(2)}, u32[]{:S(2)}) collective-permute-start(bf16[4,8,8,512]{3,2,1,0:T(8,128)(2,1)S(1)} %bitcast.6), channel_id=1, source_target_pairs={{0,1},{1,0},{2,3},{3,2},{4,5},{5,4},{6,7},{7,6},{8,9},{9,8},{10,11... | collective-permute-start | bytes 786440 | tf_op jit(solution)/shard_map/ppermute | solution.py:239
  19.3 1.6 %copy-start = (bf16[128,8192]{1,0:T(8,128)(2,1)S(1)}, bf16[128,8192]{1,0:T(8,128)(2,1)}, u32[]{:S(2)}) copy-start(bf16[128,8192]{1,0:T(8,128)(2,1)} %own_ref.1) | copy-start | bytes 6291460
  20.9 2.8 %copy-start.1 = (bf16[128,8192]{1,0:T(8,128)(2,1)S(1)}, bf16[128,8192]{1,0:T(8,128)(2,1)}, u32[]{:S(2)}) copy-start(bf16[128,8192]{1,0:T(8,128)(2,1)} %own_ref.1) | copy-start | bytes 6291460
  20.9 2.8 %copy-start.3 = (s32[32]{0:T(128)S(1)}, s32[32]{0:T(128)}, u32[]{:S(2)}) copy-start(s32[32]{0:T(128)} %param.6) | copy-start | bytes 388
  21.3 1.5 %collective-permute-start.2 = (f32[128,32]{1,0:T(8,128)S(1)}, f32[128,32]{1,0:T(8,128)S(1)}, u32[]{:S(2)}, u32[]{:S(2)}) collective-permute-start(f32[128,32]{1,0:T(8,128)S(1)} %half_logits.2.own_mine_ref), channel_id=1, source_target_pairs={{0,1},{1,0},{2,3},{3,2},{4,5},{5,4},{6,7},{7,6},{8,9},{9,8},{10,11... | collective-permute-start | bytes 49160 | tf_op jit(solution)/shard_map/ppermute | solution.py:238
  22.3 1.3 %collective-permute-start.1 = (f32[128,32]{1,0:T(8,128)S(1)}, f32[128,32]{1,0:T(8,128)S(1)}, u32[]{:S(2)}, u32[]{:S(2)}) collective-permute-start(f32[128,32]{1,0:T(8,128)S(1)} %half_logits.3.pair_mine_ref), channel_id=1, source_target_pairs={{0,1},{1,0},{2,3},{3,2},{4,5},{5,4},{6,7},{7,6},{8,9},{9,8},{10,11... | collective-permute-start | bytes 49160 | tf_op jit(solution)/shard_map/ppermute | solution.py:236
  23.6 19.1 %copy-start.4 = (s32[32]{0:T(128)S(1)}, s32[32]{0:T(128)}, u32[]{:S(2)}) copy-start(s32[32]{0:T(128)} %param.7) | copy-start | bytes 388
